TPU v7x, 32 devices: a whole 2x2x4 slice. The times are simulated.
32 devices in a mesh: req: 4 (over y, x), head: 8 (over z, core).
Axes of the slice: x: 2, y: 2, z: 4, core: 2. Of those that a mesh axis runs over, the one named last changes fastest.
Arguments:
- hidden: bfloat16 [4, 256, 5120], P('req', 'head'), may hold values from -6 to 6
- cached_len: int32 [4], P('req'), may hold values from 2 to 4096, as said below
- attn_gain: float32 [5120], replicated, may hold values from 0.5 to 1.5
- query_key_value_weight: bfloat16 [5120, 6144], P(None, 'head'), may hold values from -0.078125 to 0.078125
- b_qkv: bfloat16 [6144], P('head'), may hold values from -1.5 to 1.5
- key_cache: bfloat16 [4, 4096, 1024], P('req', 'head'), may hold values from -4000 to 4000
- value_cache: bfloat16 [4, 4096, 1024], P('req', 'head'), may hold values from -6 to 6
- w_out: bfloat16 [4096, 5120], P('head'), may hold values from -0.09375 to 0.09375
- ffn_gain: float32 [5120], replicated, may hold values from 0.5 to 1.5
- w_gate: bfloat16 [5120, 13824], P(None, 'head'), may hold values from -0.078125 to 0.078125
- w_up: bfloat16 [5120, 13824], P(None, 'head'), may hold values from -0.078125 to 0.078125
- w_down: bfloat16 [13824, 5120], P('head'), may hold values from -0.0546875 to 0.0546875
Outputs:
- layer_out: bfloat16 [4, 256, 5120], P('req', 'head')
- new_keys: bfloat16 [4, 256, 1024], P('req', 'head')
- new_values: bfloat16 [4, 256, 1024], P('req', 'head')
Inputs may be any that keep to these rules, and one draw needn't show every extreme that they name: `cached_len`: about half of the requests have nearly full caches, within 512 of 4096, one of them exactly 4096; the others hold fewer than 512 positions; which requests are which is drawn.
All inputs are finite; a program needn't handle non-finite values.
Results may differ from a plain program's by a relative error of at most 0.015.
Values may be sent and summed in bfloat16 or wider, within the bound.
A program may use at most 256 MiB of HBM per device.

v0:
```python
import math

import jax
import jax.numpy as jnp
from jax import lax
from jax.sharding import PartitionSpec as P

QUERY_HEADS = 32
KEY_VALUE_HEADS = 8
HEAD_WIDTH = 128


rope_base = 1000000.0


def rms_norm(values, gain):
    data = values.astype(jnp.float32)
    spread = jnp.mean(data * data, axis=-1, keepdims=True)
    return (data * lax.rsqrt(spread + 1e-06) * gain).astype(jnp.bfloat16)


def rope_apply(values, positions):
    half_dim = HEAD_WIDTH // 2
    inverse = rope_base ** (-(jnp.arange(half_dim, dtype=jnp.float32) * 2.0 / HEAD_WIDTH))
    angles = positions.astype(jnp.float32)[:, None] * inverse[None, :]
    cosine = jnp.concatenate([jnp.cos(angles), jnp.cos(angles)], axis=-1)[:, None, :]
    sine = jnp.concatenate([jnp.sin(angles), jnp.sin(angles)], axis=-1)[:, None, :]
    data = values.astype(jnp.float32)
    rotated = jnp.concatenate([-data[..., half_dim:], data[..., :half_dim]], axis=-1)
    return (data * cosine + rotated * sine).astype(jnp.bfloat16)


def on_device(
    hidden,
    cached_len,
    attn_gain,
    query_key_value_weight,
    b_qkv,
    key_cache,
    value_cache,
    w_out,
    ffn_gain,
    w_gate,
    w_up,
    w_down,
):
    group_size = lax.axis_size("head")
    index_here = lax.axis_index("head")
    own_rows = hidden[0]
    fresh_count = own_rows.shape[0]
    all_rows = lax.all_gather(own_rows, "head", axis=0, tiled=True)
    token_total = all_rows.shape[0]
    head_group = QUERY_HEADS // KEY_VALUE_HEADS
    heads_here = QUERY_HEADS // group_size
    scale = 1.0 / math.sqrt(HEAD_WIDTH)
    normed = rms_norm(all_rows, attn_gain)
    qkv_part = (
        jnp.dot(normed, query_key_value_weight, preferred_element_type=jnp.float32)
        + b_qkv.astype(jnp.float32)
    ).astype(jnp.bfloat16)
    query_key_value = lax.all_gather(qkv_part, "head", axis=1, tiled=True)
    query_rows = query_key_value[:, : QUERY_HEADS * HEAD_WIDTH].reshape(
        token_total, QUERY_HEADS, HEAD_WIDTH
    )
    fresh_keys = query_key_value[
        :, QUERY_HEADS * HEAD_WIDTH : (QUERY_HEADS + KEY_VALUE_HEADS) * HEAD_WIDTH
    ].reshape(token_total, KEY_VALUE_HEADS, HEAD_WIDTH)
    fresh_values = query_key_value[:, (QUERY_HEADS + KEY_VALUE_HEADS) * HEAD_WIDTH :].reshape(
        token_total, KEY_VALUE_HEADS, HEAD_WIDTH
    )
    token_ids = jnp.arange(token_total, dtype=jnp.int32)
    positions = cached_len[0] + token_ids
    query_rows = rope_apply(query_rows, positions)
    fresh_keys = rope_apply(fresh_keys, positions)
    row_start = index_here * fresh_count
    request_keys = lax.dynamic_slice_in_dim(fresh_keys, row_start, fresh_count, 0)
    request_values = lax.dynamic_slice_in_dim(fresh_values, row_start, fresh_count, 0)
    key_lines = request_keys.reshape(1, fresh_count, KEY_VALUE_HEADS * HEAD_WIDTH)
    value_lines = request_values.reshape(1, fresh_count, KEY_VALUE_HEADS * HEAD_WIDTH)
    cache_length = key_cache.shape[1]
    joined_keys = jnp.concatenate(
        [key_cache[0].reshape(cache_length, KEY_VALUE_HEADS, HEAD_WIDTH), request_keys], axis=0
    )
    joined_values = jnp.concatenate(
        [value_cache[0].reshape(cache_length, KEY_VALUE_HEADS, HEAD_WIDTH), request_values], axis=0
    )
    cache_ok = index_here * cache_length + jnp.arange(cache_length, dtype=jnp.int32) < cached_len[0]
    own_ids = row_start + jnp.arange(fresh_count, dtype=jnp.int32)
    new_ok = own_ids[None, :] <= token_ids[:, None]
    allowed = jnp.concatenate(
        [jnp.broadcast_to(cache_ok[None, :], (token_total, cache_length)), new_ok], axis=1
    )
    grouped_queries = query_rows.reshape(token_total, KEY_VALUE_HEADS, head_group, HEAD_WIDTH)
    scores = (
        jnp.einsum(
            "tkjd,skd->kjts", grouped_queries, joined_keys, preferred_element_type=jnp.float32
        )
        * scale
    )
    scores = jnp.where(allowed[None, None], scores, -1e30)
    row_max = jnp.max(scores, axis=-1)
    expo = jnp.where(allowed[None, None], jnp.exp(scores - row_max[..., None]), 0.0)
    row_sum = jnp.sum(expo, axis=-1)
    weights = expo.astype(jnp.bfloat16)
    weighted = jnp.einsum(
        "kjts,skd->tkjd", weights, joined_values, preferred_element_type=jnp.float32
    )
    weighted = weighted.reshape(token_total, QUERY_HEADS, HEAD_WIDTH)
    row_max = jnp.transpose(row_max, (2, 0, 1)).reshape(token_total, QUERY_HEADS)
    row_sum = jnp.transpose(row_sum, (2, 0, 1)).reshape(token_total, QUERY_HEADS)
    sums_got, max_got, total_got = (
        lax.all_to_all(
            weighted[None].astype(jnp.bfloat16), "head", split_axis=2, concat_axis=0, tiled=True
        ).astype(jnp.float32),
        lax.all_to_all(
            row_max[None].astype(jnp.bfloat16), "head", split_axis=2, concat_axis=0, tiled=True
        ).astype(jnp.float32),
        lax.all_to_all(
            row_sum[None].astype(jnp.bfloat16), "head", split_axis=2, concat_axis=0, tiled=True
        ).astype(jnp.float32),
    )
    joint = jnp.max(max_got, axis=0)
    factor = jnp.exp(max_got - joint[None])
    total_here = jnp.sum(total_got * factor, axis=0)
    sums_here = jnp.sum(sums_got * factor[..., None], axis=0)
    attn = (
        (sums_here / total_here[..., None])
        .astype(jnp.bfloat16)
        .reshape(token_total, heads_here * HEAD_WIDTH)
    )
    projected = jnp.dot(attn, w_out, preferred_element_type=jnp.float32)
    projected = lax.psum(projected.astype(jnp.bfloat16), "head").astype(jnp.float32)
    middle = (all_rows.astype(jnp.float32) + projected).astype(jnp.bfloat16)
    normed_two = rms_norm(middle, ffn_gain)
    middle_own = lax.dynamic_slice_in_dim(middle, row_start, fresh_count, 0)
    gate = jnp.dot(normed_two, w_gate, preferred_element_type=jnp.float32)
    upward = jnp.dot(normed_two, w_up, preferred_element_type=jnp.float32)
    active = (jax.nn.silu(gate) * upward).astype(jnp.bfloat16)
    ffn_part = lax.psum_scatter(
        jnp.dot(active, w_down, preferred_element_type=jnp.float32).astype(jnp.bfloat16),
        "head",
        scatter_dimension=0,
        tiled=True,
    ).astype(jnp.float32)
    result = (middle_own.astype(jnp.float32) + ffn_part).astype(jnp.bfloat16)
    return (result[None], key_lines, value_lines)


def solution(mesh):
    in_specs = (
        P("req", "head", None),
        P("req"),
        P(),
        P(None, "head"),
        P("head"),
        P("req", "head", None),
        P("req", "head", None),
        P("head", None),
        P(),
        P(None, "head"),
        P(None, "head"),
        P("head", None),
    )
    out_specs = (P("req", "head", None), P("req", "head", None), P("req", "head", None))
    return jax.shard_map(
        on_device, mesh=mesh, in_specs=in_specs, out_specs=out_specs, check_vma=False
    )
```

profile of v0, /device:TPU:0, one launch (start us, length us, event | category | flops | bytes accessed | tf_op | source)
XLA Modules:
  0.0 385.5 jit_solution(16978504178929794533)
XLA Ops:
  8.6 37.6 %all-gather.6.cloned.1.call-done = bf16[1,256,5120]{2,1,0:T(8,128)(2,1)} async-done(((bf16[1,32,5120]{2,1,0:T(8,128)(2,1)}), bf16[1,256,5120]{2,1,0:T(8,128)(2,1)}) %all-gather.6.cloned.1.call-update) | async-done | bytes 2621456 | tf_op jit(solution)/shard_map/all_gather | solution.py:51
  46.3 2.3 fusion.9
  48.6 7.1 %fusion.32 = bf16[256,768]{1,0:T(8,128)(2,1)} fusion(bf16[5120,768]{1,0:T(8,128)(2,1)} %param.15, bf16[1,256,5120]{2,1,0:T(8,128)(2,1)} %all-gather.6.cloned.1.call-done, f32[5120]{0:T(1024)} %param.14, f32[256]{0:T(256)S(1)} %add_rsqrt_fusion.1, f32[768]{0:T(1024)S(1)} %convert_element_type.173), kind=kOutput, calls=%fused_computation.40 | convolution fusion | flops 2018902016 | bytes 10903552 | tf_op jit(solution)/shard_map/dot_general | solution.py:58
  57.0 1.3 copy.73
  58.9 1.3 copy.68
  62.4 30.8 %all-gather.4.cloned.1.call-done = bf16[256,6144]{1,0:T(8,128)(2,1)} async-done(((bf16[256,768]{1,0:T(8,128)(2,1)}), bf16[256,6144]{1,0:T(8,128)(2,1)}) %all-gather.4.cloned.1.call-update) | async-done | bytes 3145744 | tf_op jit(solution)/shard_map/all_gather | solution.py:61
  93.2 2.3 slice_bitcast_fusion
  96.7 2.5 slice_convert_fusion
  99.1 5.6 %copy.75 = f32[256,4096]{0,1:T(8,128)} copy(f32[256,4096]{1,0:T(8,128)} %slice_convert_fusion) | data formatting | bytes 8388608 | tf_op jit(solution)/shard_map/convert_element_type | solution.py:28
  104.7 6.0 %reshape.139 = f32[256,8,4,128]{3,2,1,0:T(4,128)} reshape(f32[256,4096]{1,0:T(8,128)} %slice_convert_fusion) | data formatting | bytes 8388608 | tf_op jit(solution)/shard_map/convert_element_type | solution.py:28
  111.0 1.2 copy_negate_fusion
  112.2 1.2 copy-done
  113.3 1.7 slice_negate_fusion
  115.1 3.8 copy.76
  118.9 2.8 copy.77
  121.7 1.1 fusion.46
  122.8 13.2 %fusion = (f32[8,4,256]{2,1,0:T(4,128)S(1)}, f32[8,544,256,4]{2,1,3,0:T(8,128)}) fusion(pred[256,544]{0,1:T(8,128)(4,1)S(1)} %pad_add_fusion, f32[256,8,4,64]{3,0,2,1:T(8,128)} %copy.77, f32[256,8,4,64]{3,0,2,1:T(8,128)} %copy.76, f32[256,8,4,128]{3,2,1,0:T(4,128)} %reshape.139, f32[256,128]{1,0:T(8,128)S(1)} %get-tuple-element.18, ...), kind=kOutput, calls=%fused_computation.2 | convolution fusion | flops 1161682944 | bytes 27762688 | tf_op jit(solution)/shard_map/tkjd,skd->kjts/dot_general | solution.py:95
  136.1 10.5 %fusion.1 = bf16[8,4,256]{2,1,0:T(4,128)(2,1)S(1)} fusion(f32[8,544,256,4]{2,1,3,0:T(8,128)} %get-tuple-element.16, f32[8,4,256]{2,1,0:T(4,128)S(1)} %get-tuple-element.15, pred[256,544]{0,1:T(8,128)(4,1)S(1)} %pad_add_fusion), kind=kLoop, calls=%fused_computation.3 | loop fusion | flops 22274048 | bytes 18014208 | tf_op jit(solution)/shard_map/reduce_sum | solution.py:103
  148.5 3.3 all-to-all-start.2
  153.3 4.1 %all-to-all-done.2 = bf16[8,2,512]{2,1,0:T(2,128)(2,1)S(1)} async-done(((bf16[8,2,512]{2,1,0:T(2,128)(2,1)}), bf16[8,2,512]{2,1,0:T(2,128)(2,1)S(1)}, u32[]{:S(2)}, u32[]{:S(2)}) %all-to-all-start.2) | async-done | bytes 16416 | tf_op jit(solution)/shard_map/all_to_all | solution.py:118
  157.4 3.3 all-to-all-start.1
  160.7 9.4 %fusion.26 = bf16[8,128,4,256]{3,1,2,0:T(8,128)(2,1)} fusion(f32[8,544,256,4]{2,1,3,0:T(8,128)} %get-tuple-element.16, f32[8,4,256]{2,1,0:T(4,128)S(1)} %get-tuple-element.15, pred[256,544]{0,1:T(8,128)(4,1)S(1)} %pad_add_fusion, bf16[32,8,128]{2,0,1:T(8,128)(2,1)S(1)} %copy.87, bf16[512,8,128]{2,0,1:T(8,128)(2,1)S(1)} %copy-done.7), kind=kOutput, calls=%fused_computation.38 | convolution fusion | flops 1166409728 | bytes 21209088 | tf_op jit(solution)/shard_map/kjts,skd->tkjd/dot_general | solution.py:105
  170.2 5.0 %all-to-all-start = ((bf16[1,256,32,128]{1,3,0,2:T(8,128)(2,1)}), bf16[1,256,32,128]{1,3,0,2:T(8,128)(2,1)S(1)}, u32[]{:S(2)}, u32[]{:S(2)}) async-start(bf16[1,256,32,128]{1,3,0,2:T(8,128)(2,1)} %bitcast.122), calls=%async_computation | async-start | bytes 4194304 | tf_op jit(solution)/shard_map/all_to_all | solution.py:112
  175.6 48.7 %all-to-all-done = bf16[1,256,32,128]{1,3,0,2:T(8,128)(2,1)S(1)} async-done(((bf16[1,256,32,128]{1,3,0,2:T(8,128)(2,1)}), bf16[1,256,32,128]{1,3,0,2:T(8,128)(2,1)S(1)}, u32[]{:S(2)}, u32[]{:S(2)}) %all-to-all-start) | async-done | bytes 2097184 | tf_op jit(solution)/shard_map/all_to_all | solution.py:112
  224.7 5.7 %convolution_convert_fusion.1 = bf16[256,5120]{1,0:T(8,128)(2,1)} fusion(bf16[256,512]{0,1:T(8,128)(2,1)S(1)} %bitcast.123, bf16[512,5120]{1,0:T(8,128)(2,1)} %param.19), kind=kOutput, calls=%fused_computation.13 | convolution fusion | flops 1343488000 | bytes 8126464 | tf_op jit(solution)/shard_map/dot_general | solution.py:131
  230.5 68.1 %all-reduce.2.cloned.1.call-done = bf16[256,5120]{1,0:T(8,128)(2,1)} async-done(((bf16[256,5120]{1,0:T(8,128)(2,1)}), bf16[256,5120]{1,0:T(8,128)(2,1)}) %all-reduce.2.cloned.1.call-update) | async-done | bytes 2621456 | tf_op jit(solution)/shard_map/psum | solution.py:132
  298.7 2.9 fusion.6
  301.7 1.5 copy-done.2
  303.1 8.9 %fusion.40 = f32[256,1728]{0,1:T(8,128)S(1)} fusion(bf16[5120,1728]{0,1:T(8,128)(2,1)} %param.21, bf16[256,5120]{1,0:T(8,128)(2,1)S(1)} %get-tuple-element.4, f32[5120]{0:T(1024)S(1)} %copy-done.10, f32[256]{0:T(256)S(1)} %add_rsqrt_fusion), kind=kOutput, calls=%fused_computation.51 | convolution fusion | flops 4535091200 | bytes 22107136 | tf_op jit(solution)/shard_map/dot_general | solution.py:136
  312.0 28.5 %convolution_convert_fusion = bf16[256,5120]{1,0:T(8,128)(2,1)} fusion(bf16[1728,5120]{1,0:T(8,128)(2,1)} %param.23, bf16[5120,1728]{0,1:T(8,128)(2,1)} %param.22, f32[256,1728]{0,1:T(8,128)S(1)} %fusion.40, bf16[256,5120]{1,0:T(8,128)(2,1)} %copy-done.2, f32[5120]{0:T(1024)S(1)} %copy-done.10, f32[256]{0:T(256)S(1)} %add_rsqrt_fusion), kind=kOutput, calls=%fused_computation.12 | convolution fusion | flops 9068904448 | bytes 42423296 | tf_op jit(solution)/shard_map/dot_general | solution.py:140
  341.9 35.2 %reduce-scatter.2.cloned.1.call-done = bf16[32,5120]{1,0:T(8,128)(2,1)} async-done(((bf16[256,5120]{1,0:T(8,128)(2,1)}), bf16[32,5120]{1,0:T(8,128)(2,1)}) %reduce-scatter.2.cloned.1.call-update) | async-done | bytes 327696 | tf_op jit(solution)/shard_map/reduce_scatter | solution.py:139
  377.1 1.9 fusion.42
  (74 shorter events, 11.8 us)
Async XLA Ops:
  7.2 39.1 %all-gather.6.cloned.1.call-start = ((), (), s32[]{:S(2)}) async-start(), calls=%async_computation.7 | async-start | bytes 2949120 | tf_op jit(solution)/shard_map/all_gather | solution.py:51
  7.9 85.3 %all-gather.4.cloned.1.call-start = ((), (), s32[]{:S(2)}) async-start(), calls=%async_computation.4 | async-start | bytes 3538944 | tf_op jit(solution)/shard_map/all_gather | solution.py:61
  48.6 7.9 %copy-start.5 = (bf16[1,512,1024]{2,1,0:T(8,128)(2,1)S(1)}, bf16[1,512,1024]{2,1,0:T(8,128)(2,1)}, u32[]{:S(2)}) copy-start(bf16[1,512,1024]{2,1,0:T(8,128)(2,1)} %param.17) | copy-start | bytes 3145732
  55.7 2.6 copy-start.6
  93.2 3.5 copy-start.3
  110.8 2.6 copy-start
  122.8 13.2 %copy-start.8 = (bf16[32,8,128]{2,0,1:T(8,128)(2,1)}, bf16[32,8,128]{2,0,1:T(8,128)(2,1)S(1)}, u32[]{:S(2)}) copy-start(bf16[32,8,128]{2,0,1:T(8,128)(2,1)S(1)} %fusion.46) | copy-start | bytes 196612
  136.1 15.7 %copy-start.4 = (bf16[32,8,8,128]{3,1,2,0:T(8,128)(2,1)S(1)}, bf16[32,8,8,128]{3,1,2,0:T(8,128)(2,1)}, u32[]{:S(2)}) copy-start(bf16[32,8,8,128]{3,1,2,0:T(8,128)(2,1)} %get-tuple-element.7) | copy-start | bytes 1572868
  136.1 24.6 %copy-start.7 = (bf16[512,8,128]{2,0,1:T(8,128)(2,1)S(1)}, bf16[512,8,128]{2,0,1:T(8,128)(2,1)}, u32[]{:S(2)}) copy-start(bf16[512,8,128]{2,0,1:T(8,128)(2,1)} %copy.68) | copy-start | bytes 3145732
  148.5 8.9 %all-to-all-start.2 = ((bf16[8,2,512]{2,1,0:T(2,128)(2,1)}), bf16[8,2,512]{2,1,0:T(2,128)(2,1)S(1)}, u32[]{:S(2)}, u32[]{:S(2)}) async-start(bf16[8,2,512]{2,1,0:T(2,128)(2,1)} %reshape.155), calls=%async_computation.2 | async-start | bytes 32768 | tf_op jit(solution)/shard_map/all_to_all | solution.py:118
  157.4 12.8 %all-to-all-start.1 = ((bf16[8,2,512]{2,1,0:T(2,128)(2,1)}), bf16[8,2,512]{2,1,0:T(2,128)(2,1)S(1)}, u32[]{:S(2)}, u32[]{:S(2)}) async-start(bf16[8,2,512]{2,1,0:T(2,128)(2,1)} %reshape.153), calls=%async_computation.1 | async-start | bytes 32768 | tf_op jit(solution)/shard_map/all_to_all | solution.py:115
  170.2 54.1 %all-to-all-start = ((bf16[1,256,32,128]{1,3,0,2:T(8,128)(2,1)}), bf16[1,256,32,128]{1,3,0,2:T(8,128)(2,1)S(1)}, u32[]{:S(2)}, u32[]{:S(2)}) async-start(bf16[1,256,32,128]{1,3,0,2:T(8,128)(2,1)} %bitcast.122), calls=%async_computation | async-start | bytes 4194304 | tf_op jit(solution)/shard_map/all_to_all | solution.py:112
  175.2 123.5 %all-reduce.2.cloned.1.call-start = ((), (), s32[]{:S(2)}) async-start(), calls=%async_computation.5 | async-start | bytes 5242880 | tf_op jit(solution)/shard_map/psum | solution.py:132
  224.7 74.0 %copy-start.1 = (bf16[1,256,5120]{2,1,0:T(8,128)(2,1)S(1)}, bf16[1,256,5120]{2,1,0:T(8,128)(2,1)}, u32[]{:S(2)}) copy-start(bf16[1,256,5120]{2,1,0:T(8,128)(2,1)} %all-gather.6.cloned.1.call-done) | copy-start | bytes 7864324
  230.5 72.7 %copy-start.10 = (f32[5120]{0:T(1024)S(1)}, f32[5120]{0:T(1024)}, u32[]{:S(2)}) copy-start(f32[5120]{0:T(1024)} %param.20) | copy-start | bytes 61444
  230.5 146.6 %reduce-scatter.2.cloned.1.call-start = ((), (), s32[]{:S(2)}) async-start(), calls=%async_computation.6 | async-start | bytes 2949120 | tf_op jit(solution)/shard_map/reduce_scatter | solution.py:139
  301.6 1.5 copy-start.2
  312.0 28.5 %copy-start.9 = (bf16[32,8,128]{2,0,1:T(8,128)(2,1)S(1)}, bf16[32,8,128]{2,0,1:T(8,128)(2,1)}, u32[]{:S(2)}) copy-start(bf16[32,8,128]{2,0,1:T(8,128)(2,1)} %copy-done.8) | copy-start | bytes 196612
Sparse Core Ops, SparseCore 0:
  9.6 36.5 all-gather.5
  55.9 37.2 all-gather.3
  230.6 68.0 all-reduce.1
  340.6 36.4 reduce-scatter.1
where the time goes:
time: 386 us; the launch traced here: 385 us
  waiting for transfers between devices  225 us (58%)
  matrix products  72.8 us (19%)
  local copies, waits for them, and re-layouts  30.7 us (8%)
  other arithmetic  30.1 us (8%)
  between operations  14.8 us (4%)
  starting transfers between devices  11.8 us (3%)
    psum x1, waiting for transfers between devices, on_device(): lax.psum(projected.astype(jnp.bfloat16), 'head').astype(jnp.float32)  68.1 us
    all_to_all x1, waiting for transfers between devices, on_device(): lax.all_to_all(weighted[None].astype(jnp.bfloat16), 'head', split_axis=2,...  48.7 us
    all_gather x1, waiting for transfers between devices, on_device(): all_rows = lax.all_gather(own_rows, 'head', axis=0, tiled=True)  37.6 us
    reduce_scatter x1, waiting for transfers between devices, on_device(): lax.psum_scatter(jnp.dot(active, w_down, preferred_element_type=jnp.float...  35.2 us
    all_gather x1, waiting for transfers between devices, on_device(): query_key_value = lax.all_gather(qkv_part, 'head', axis=1, tiled=True)  30.8 us
    dot_general x1, matrix products, on_device(): jnp.dot(active, w_down, preferred_element_type=jnp.float32)  28.5 us
    dot_general x1, matrix products, on_device(): jnp.einsum('tkjd,skd->kjts', grouped_queries, joined_keys, preferred_elem...  13.2 us
    convert_element_type x2, local copies, waits for them, and re-layouts, rope_apply(): data = values.astype(jnp.float32)  11.6 us
  transfers between devices with their start and end apart: 7, of which 6 were waited for; matrix products, arithmetic and copies ran while one was open for 5% of the time, Pallas kernels for 0%

commit v1 on v0

v1 whole, which is shorter than its diff:
```python
import functools
import math

import jax
import jax.numpy as jnp
from jax import lax
from jax.experimental import pallas as pl
from jax.experimental.pallas import tpu as pltpu
from jax.sharding import PartitionSpec as P

QUERY_HEADS = 32
KEY_VALUE_HEADS = 8
HEAD_WIDTH = 128
GROUP = QUERY_HEADS // KEY_VALUE_HEADS
SCALE = 1.0 / math.sqrt(HEAD_WIDTH)
TAIL = 16

rope_base = 1000000.0
MESH = pl.DeviceIdType.MESH


def rms_norm(values, gain):
    data = values.astype(jnp.float32)
    spread = jnp.mean(data * data, axis=-1, keepdims=True)
    return (data * lax.rsqrt(spread + 1e-06) * gain).astype(jnp.bfloat16)


def rope_tables(positions):
    half_dim = HEAD_WIDTH // 2
    inverse = rope_base ** (-(jnp.arange(half_dim, dtype=jnp.float32) * 2.0 / HEAD_WIDTH))
    angles = positions.astype(jnp.float32)[:, None] * inverse[None, :]
    cosine = jnp.cos(angles)
    sine = jnp.sin(angles)
    return (
        jnp.concatenate([cosine, cosine], axis=-1),
        jnp.concatenate([-sine, sine], axis=-1),
    )


def chain_barrier(chips, me, chip, partner):
    barrier = pltpu.get_barrier_semaphore()
    pl.semaphore_signal(barrier, inc=1, device_id={"head": partner}, device_id_type=MESH)

    @pl.when(chip > 0)
    def _():
        pl.semaphore_signal(barrier, inc=1, device_id={"head": me - 2}, device_id_type=MESH)

    @pl.when(chip < chips - 1)
    def _():
        pl.semaphore_signal(barrier, inc=1, device_id={"head": me + 2}, device_id_type=MESH)

    below = (chip + chips - 1) // chips
    above = (2 * chips - 2 - chip) // chips
    pl.semaphore_wait(barrier, 1 + below + above)


def gather_kernel(chips, x_ref, out_ref, own_sem, up_send, down_send, chip_recv, pair_send, pair_recv):
    me = lax.axis_index("head")
    chip = me // 2
    core = me % 2
    partner = chip * 2 + (1 - core)
    chain_barrier(chips, me, chip, partner)

    def to_up(src, owner):
        return pltpu.make_async_remote_copy(
            src_ref=src,
            dst_ref=out_ref.at[owner * 2 + core],
            send_sem=up_send.at[owner],
            recv_sem=chip_recv.at[owner],
            device_id={"head": me + 2},
            device_id_type=MESH,
        )

    def to_down(src, owner):
        return pltpu.make_async_remote_copy(
            src_ref=src,
            dst_ref=out_ref.at[owner * 2 + core],
            send_sem=down_send.at[owner],
            recv_sem=chip_recv.at[owner],
            device_id={"head": me - 2},
            device_id_type=MESH,
        )

    def to_partner(src, owner):
        return pltpu.make_async_remote_copy(
            src_ref=src,
            dst_ref=out_ref.at[owner * 2 + core],
            send_sem=pair_send.at[owner],
            recv_sem=pair_recv.at[owner],
            device_id={"head": partner},
            device_id_type=MESH,
        )

    @pl.when(chip < chips - 1)
    def _():
        to_up(x_ref, chip).start()

    @pl.when(chip > 0)
    def _():
        to_down(x_ref, chip).start()

    to_partner(x_ref, chip).start()
    own = pltpu.make_async_copy(x_ref, out_ref.at[me], own_sem)
    own.start()

    def step(s, carry):
        @pl.when(chip - s >= 0)
        def _():
            owner = chip - s
            held = out_ref.at[owner * 2 + core]
            to_up(held, owner).wait_recv()

            @pl.when(chip < chips - 1)
            def _():
                to_up(held, owner).start()

            to_partner(held, owner).start()

        @pl.when(chip + s <= chips - 1)
        def _():
            owner = chip + s
            held = out_ref.at[owner * 2 + core]
            to_down(held, owner).wait_recv()

            @pl.when(chip > 0)
            def _():
                to_down(held, owner).start()

            to_partner(held, owner).start()

        return carry

    lax.fori_loop(1, chips, step, 0)
    own.wait()

    def finish(owner, carry):
        to_partner(x_ref, owner).wait()

        @pl.when((chip < chips - 1) & (owner <= chip))
        def _():
            to_up(x_ref, owner).wait_send()

        @pl.when((chip > 0) & (owner >= chip))
        def _():
            to_down(x_ref, owner).wait_send()

        return carry

    lax.fori_loop(0, chips, finish, 0)


def gather(x, size, collective_id):
    chips = size // 2
    return pl.pallas_call(
        functools.partial(gather_kernel, chips),
        out_shape=jax.ShapeDtypeStruct((size,) + x.shape, x.dtype),
        in_specs=[pl.BlockSpec(memory_space=pl.ANY)],
        out_specs=pl.BlockSpec(memory_space=pl.ANY),
        scratch_shapes=[pltpu.SemaphoreType.DMA(())] + [pltpu.SemaphoreType.DMA((chips,))] * 5,
        compiler_params=pltpu.CompilerParams(collective_id=collective_id, has_side_effects=True),
        name="gather%d" % collective_id,
    )(x)


def scatter_kernel(
    chips, x_ref, out_ref, pair, up, down, pair_send, pair_recv, up_send, up_recv, down_send, down_recv
):
    me = lax.axis_index("head")
    chip = me // 2
    core = me % 2
    partner = chip * 2 + (1 - core)
    half = chip // (chips // 2)
    chain_barrier(chips, me, chip, partner)

    def to_partner(j):
        return pltpu.make_async_remote_copy(
            src_ref=x_ref.at[2 * j + (1 - core)],
            dst_ref=pair.at[j],
            send_sem=pair_send.at[j],
            recv_sem=pair_recv.at[j],
            device_id={"head": partner},
            device_id_type=MESH,
        )

    def to_up(src, j):
        return pltpu.make_async_remote_copy(
            src_ref=src,
            dst_ref=up.at[j],
            send_sem=up_send.at[j],
            recv_sem=up_recv.at[j],
            device_id={"head": me + 2},
            device_id_type=MESH,
        )

    def to_down(src, j):
        return pltpu.make_async_remote_copy(
            src_ref=src,
            dst_ref=down.at[j],
            send_sem=down_send.at[j],
            recv_sem=down_recv.at[j],
            device_id={"head": me - 2},
            device_id_type=MESH,
        )

    def order(k):
        return (1 - half) * (chips - 1 - k) + half * k

    def first(k, carry):
        to_partner(order(k)).start()
        return carry

    lax.fori_loop(0, chips, first, 0)

    def second(k, carry):
        j = order(k)
        to_partner(j).wait_recv()
        pair[j] = pair[j] + x_ref[2 * j + core]

        @pl.when((chip == 0) & (j > 0))
        def _():
            to_up(pair.at[j], j).start()

        @pl.when((chip == chips - 1) & (j < chips - 1))
        def _():
            to_down(pair.at[j], j).start()

        return carry

    lax.fori_loop(0, chips, second, 0)

    def move_up(j):
        @pl.when((chip > 0) & (j > chip))
        def _():
            to_up(up.at[j], j).wait_recv()
            up[j] = up[j] + pair[j]
            to_up(up.at[j], j).start()

    def move_down(j):
        @pl.when((chip < chips - 1) & (j < chip))
        def _():
            to_down(down.at[j], j).wait_recv()
            down[j] = down[j] + pair[j]
            to_down(down.at[j], j).start()

    def third(s, carry):
        @pl.when(half == 0)
        def _():
            move_up(chips - 1 - s)

        move_down(s)

        @pl.when(half == 1)
        def _():
            move_up(chips - 1 - s)

        return carry

    lax.fori_loop(0, chips - 1, third, 0)
    out_ref[...] = pair[chip].astype(jnp.float32)

    @pl.when(chip > 0)
    def _():
        to_up(up.at[chip], chip).wait_recv()
        out_ref[...] = out_ref[...] + up[chip].astype(jnp.float32)

    @pl.when(chip < chips - 1)
    def _():
        to_down(down.at[chip], chip).wait_recv()
        out_ref[...] = out_ref[...] + down[chip].astype(jnp.float32)

    def finish(j, carry):
        to_partner(j).wait_send()

        @pl.when(j > chip)
        def _():
            to_up(pair.at[j], j).wait_send()

        @pl.when(j < chip)
        def _():
            to_down(pair.at[j], j).wait_send()

        return carry

    lax.fori_loop(0, chips, finish, 0)


def scatter(x, size, collective_id):
    chips = size // 2
    shape = x.shape[1:]
    return pl.pallas_call(
        functools.partial(scatter_kernel, chips),
        out_shape=jax.ShapeDtypeStruct(shape, jnp.float32),
        in_specs=[pl.BlockSpec(memory_space=pltpu.VMEM)],
        out_specs=pl.BlockSpec(memory_space=pltpu.VMEM),
        scratch_shapes=[pltpu.VMEM((chips,) + shape, x.dtype)] * 3
        + [pltpu.SemaphoreType.DMA((chips,))] * 6,
        compiler_params=pltpu.CompilerParams(
            collective_id=collective_id, has_side_effects=True, vmem_limit_bytes=24 << 20
        ),
        name="scatter%d" % collective_id,
    )(x)


def factor_kernel(size, x_ref, out_ref, held, send_sem, recv_sem):
    me = lax.axis_index("head")
    barrier = pltpu.get_barrier_semaphore()

    def greet(k, carry):
        pl.semaphore_signal(
            barrier, inc=1, device_id={"head": (me + k) % size}, device_id_type=MESH
        )
        return carry

    lax.fori_loop(1, size, greet, 0)
    pl.semaphore_wait(barrier, size - 1)

    def copy(slot, other):
        return pltpu.make_async_remote_copy(
            src_ref=x_ref,
            dst_ref=held.at[slot],
            send_sem=send_sem.at[other],
            recv_sem=recv_sem.at[slot],
            device_id={"head": other},
            device_id_type=MESH,
        )

    def start(k, carry):
        copy(me, (me + k) % size).start()
        return carry

    lax.fori_loop(1, size, start, 0)

    def collect(k, best):
        other = (me + k) % size
        copy(other, other).wait_recv()
        return jnp.maximum(best, held[other])

    own = x_ref[...]
    best = lax.fori_loop(1, size, collect, own)
    out_ref[...] = jnp.exp((own - best) * SCALE)

    def finish(k, carry):
        copy(me, (me + k) % size).wait_send()
        return carry

    lax.fori_loop(1, size, finish, 0)


def joint_factor(x, size, collective_id):
    return pl.pallas_call(
        functools.partial(factor_kernel, size),
        out_shape=jax.ShapeDtypeStruct(x.shape, jnp.float32),
        in_specs=[pl.BlockSpec(memory_space=pltpu.VMEM)],
        out_specs=pl.BlockSpec(memory_space=pltpu.VMEM),
        scratch_shapes=[
            pltpu.VMEM((size,) + x.shape, x.dtype),
            pltpu.SemaphoreType.DMA((size,)),
            pltpu.SemaphoreType.DMA((size,)),
        ],
        compiler_params=pltpu.CompilerParams(collective_id=collective_id, has_side_effects=True),
        name="factor%d" % collective_id,
    )(x)


def attend_kernel(info_ref, q_ref, kc_ref, vc_ref, kn_ref, vn_ref, cos_ref, sin_ref, sum_ref, max_ref):
    tokens = q_ref.shape[0]
    length = kc_ref.shape[0]
    fresh = kn_ref.shape[0]
    width = GROUP * tokens
    cosine = cos_ref[...]
    sine = sin_ref[...]
    parts = []
    for j in range(GROUP):
        data = q_ref[:, j * HEAD_WIDTH : (j + 1) * HEAD_WIDTH].astype(jnp.float32)
        turned = pltpu.roll(data, HEAD_WIDTH // 2, 1)
        parts.append((data * cosine + turned * sine).astype(jnp.bfloat16))
    query = jnp.concatenate(parts, axis=0)
    last = (((1,), (1,)), ((), ()))
    first = (((0,), (0,)), ((), ()))
    old = lax.dot_general(kc_ref[...], query, last, preferred_element_type=jnp.float32)
    new = lax.dot_general(kn_ref[...], query, last, preferred_element_type=jnp.float32)
    old_ids = lax.broadcasted_iota(jnp.int32, (length, 1), 0)
    old = jnp.where(old_ids < info_ref[0], old, -1e30)
    new_ids = lax.broadcasted_iota(jnp.int32, (fresh, width), 0) + info_ref[1]
    token_ids = lax.broadcasted_iota(jnp.int32, (fresh, width), 1) % tokens
    new = jnp.where(new_ids <= token_ids, new, -1e30)
    top = jnp.maximum(jnp.max(old, axis=0, keepdims=True), jnp.max(new, axis=0, keepdims=True))
    top = jnp.maximum(top, -1e29)
    old = jnp.exp((old - top) * SCALE)
    new = jnp.exp((new - top) * SCALE)
    total = jnp.sum(old, axis=0, keepdims=True) + jnp.sum(new, axis=0, keepdims=True)
    sums = lax.dot_general(
        vc_ref[...], old.astype(jnp.bfloat16), first, preferred_element_type=jnp.float32
    ) + lax.dot_general(
        vn_ref[...], new.astype(jnp.bfloat16), first, preferred_element_type=jnp.float32
    )
    sum_ref[0, :HEAD_WIDTH, :] = sums.astype(jnp.bfloat16)
    sum_ref[0, HEAD_WIDTH:, :] = jnp.broadcast_to(total, (TAIL, width)).astype(jnp.bfloat16)
    max_ref[pl.ds(pl.program_id(0), 1), :] = top


def attend(info, qkv, key_cache, value_cache, new_keys, new_values, cosine, sine):
    tokens = qkv.shape[0]
    length = key_cache.shape[0]
    fresh = new_keys.shape[0]
    width = GROUP * tokens

    def head_block(rows):
        return pl.BlockSpec((rows, HEAD_WIDTH), lambda g, info: (0, g))

    def whole_block(shape):
        return pl.BlockSpec(shape, lambda g, info: (0, 0))

    return pl.pallas_call(
        attend_kernel,
        grid_spec=pltpu.PrefetchScalarGridSpec(
            num_scalar_prefetch=1,
            grid=(KEY_VALUE_HEADS,),
            in_specs=[
                pl.BlockSpec((tokens, GROUP * HEAD_WIDTH), lambda g, info: (0, g)),
                head_block(length),
                head_block(length),
                head_block(fresh),
                head_block(fresh),
                whole_block((tokens, HEAD_WIDTH)),
                whole_block((tokens, HEAD_WIDTH)),
            ],
            out_specs=[
                pl.BlockSpec((1, HEAD_WIDTH + TAIL, width), lambda g, info: (g, 0, 0)),
                whole_block((KEY_VALUE_HEADS, width)),
            ],
        ),
        out_shape=[
            jax.ShapeDtypeStruct((KEY_VALUE_HEADS, HEAD_WIDTH + TAIL, width), jnp.bfloat16),
            jax.ShapeDtypeStruct((KEY_VALUE_HEADS, width), jnp.float32),
        ],
        compiler_params=pltpu.CompilerParams(
            dimension_semantics=("arbitrary",), vmem_limit_bytes=32 << 20
        ),
        name="attend",
    )(info, qkv, key_cache, value_cache, new_keys, new_values, cosine, sine)


def on_device(
    hidden,
    cached_len,
    attn_gain,
    query_key_value_weight,
    b_qkv,
    key_cache,
    value_cache,
    w_out,
    ffn_gain,
    w_gate,
    w_up,
    w_down,
):
    size = lax.axis_size("head")
    index_here = lax.axis_index("head")
    own_rows = hidden[0]
    fresh, model = own_rows.shape
    tokens = fresh * size
    heads_here = QUERY_HEADS // size
    row_start = index_here * fresh
    cache_length = key_cache.shape[1]
    key_start = QUERY_HEADS * HEAD_WIDTH

    cosine, sine = rope_tables(cached_len[0] + jnp.arange(tokens, dtype=jnp.int32))
    own_cosine = lax.dynamic_slice_in_dim(cosine, row_start, fresh, 0)[:, None, :]
    own_sine = lax.dynamic_slice_in_dim(sine, row_start, fresh, 0)[:, None, :]

    normed = gather(rms_norm(own_rows, attn_gain), size, 0).reshape(tokens, model)
    qkv_part = (
        jnp.dot(normed, query_key_value_weight, preferred_element_type=jnp.float32)
        + b_qkv.astype(jnp.float32)
    ).astype(jnp.bfloat16)
    qkv = jnp.transpose(gather(qkv_part, size, 1), (1, 0, 2)).reshape(tokens, -1)
    own = lax.dynamic_slice(
        qkv, (row_start, key_start), (fresh, 2 * KEY_VALUE_HEADS * HEAD_WIDTH)
    )
    key_data = own[:, : KEY_VALUE_HEADS * HEAD_WIDTH].astype(jnp.float32)
    key_data = key_data.reshape(fresh, KEY_VALUE_HEADS, HEAD_WIDTH)
    turned = jnp.roll(key_data, HEAD_WIDTH // 2, axis=-1)
    new_keys = (key_data * own_cosine + turned * own_sine).astype(jnp.bfloat16)
    new_keys = new_keys.reshape(fresh, KEY_VALUE_HEADS * HEAD_WIDTH)
    new_values = own[:, KEY_VALUE_HEADS * HEAD_WIDTH :]

    info = jnp.stack([cached_len[0] - index_here * cache_length, row_start]).astype(jnp.int32)
    sums, tops = attend(
        info, qkv, key_cache[0], value_cache[0], new_keys, new_values, cosine, sine
    )
    factor = joint_factor(tops, size, 2)
    sums = (sums.astype(jnp.float32) * factor[:, None, :]).astype(jnp.bfloat16)
    split = size // KEY_VALUE_HEADS
    width = heads_here * tokens
    sums = jnp.transpose(
        sums.reshape(KEY_VALUE_HEADS, HEAD_WIDTH + TAIL, split, width), (0, 2, 1, 3)
    ).reshape(size, HEAD_WIDTH + TAIL, width)
    mixed = scatter(sums, size, 3)
    attn = (mixed[:HEAD_WIDTH] / mixed[HEAD_WIDTH : HEAD_WIDTH + 1]).astype(jnp.bfloat16)
    attn = jnp.transpose(attn.reshape(HEAD_WIDTH, heads_here, tokens), (2, 1, 0))
    attn = attn.reshape(tokens, heads_here * HEAD_WIDTH)
    projected = jnp.dot(attn, w_out, preferred_element_type=jnp.float32).astype(jnp.bfloat16)
    projected = scatter(projected.reshape(size, fresh, model), size, 4)
    middle = (own_rows.astype(jnp.float32) + projected).astype(jnp.bfloat16)
    normed_two = gather(rms_norm(middle, ffn_gain), size, 5).reshape(tokens, model)
    gate = jnp.dot(normed_two, w_gate, preferred_element_type=jnp.float32)
    upward = jnp.dot(normed_two, w_up, preferred_element_type=jnp.float32)
    active = (jax.nn.silu(gate) * upward).astype(jnp.bfloat16)
    active = lax.optimization_barrier(active)
    ffn_part = jnp.dot(active, w_down, preferred_element_type=jnp.float32).astype(jnp.bfloat16)
    ffn_sum = scatter(ffn_part.reshape(size, fresh, model), size, 6)
    result = (middle.astype(jnp.float32) + ffn_sum).astype(jnp.bfloat16)
    return (result[None], new_keys[None], new_values[None])


def solution(mesh):
    in_specs = (
        P("req", "head", None),
        P("req"),
        P(),
        P(None, "head"),
        P("head"),
        P("req", "head", None),
        P("req", "head", None),
        P("head", None),
        P(),
        P(None, "head"),
        P(None, "head"),
        P("head", None),
    )
    out_specs = (P("req", "head", None), P("req", "head", None), P("req", "head", None))
    return jax.shard_map(
        on_device, mesh=mesh, in_specs=in_specs, out_specs=out_specs, check_vma=False
    )
```

time: 386 us -> 253 us (0.66)
  waiting for transfers between devices: 225 us -> 0 us
  Pallas kernels: 0 us -> 199 us
  matrix products: 72.8 us -> 39.3 us
  local copies, waits for them, and re-layouts: 30.7 us -> 4.9 us
  other arithmetic: 30.1 us -> 8.36 us
  between operations: 14.8 us -> 1.68 us
  starting transfers between devices: 11.8 us -> 0 us
    pallas_call x0 -> x8, Pallas kernels: none -> 199 us  [the longest x3 93.8 us: gather(): pl.pallas_call(functools.partial(gather_kernel, chips), out_shape=jax.Sha...]
    all_gather x2 -> x0, waiting for transfers between devices: 68.4 us -> none  [the longest x1 37.6 us: on_device(): all_rows = lax.all_gather(own_rows, 'head', axis=0, tiled=True)]
    psum x1 -> x0, waiting for transfers between devices: 68.1 us -> none  [on_device(): lax.psum(projected.astype(jnp.bfloat16), 'head').astype(jnp.float32)]
    all_to_all x3 -> x0, waiting for transfers between devices: 52.7 us -> none  [the longest x1 48.7 us: on_device(): lax.all_to_all(weighted[None].astype(jnp.bfloat16), 'head', split_axis=2,...]
    reduce_scatter x1 -> x0, waiting for transfers between devices: 35.2 us -> none  [on_device(): lax.psum_scatter(jnp.dot(active, w_down, preferred_element_type=jnp.float...]
    dot_general x1, matrix products: 28.5 us -> 5.36 us  [on_device(): jnp.dot(active, w_down, preferred_element_type=jnp.float32)]
    dot_general x3 -> x2, matrix products: 28.3 us -> 13.7 us  [the longest x1 9.67 us: on_device(): upward = jnp.dot(normed_two, w_up, preferred_element_type=jnp.float32)]
    all_to_all x3 -> x0, starting transfers between devices: 11.7 us -> none  [the longest x1 5.02 us: on_device(): lax.all_to_all(weighted[None].astype(jnp.bfloat16), 'head', split_axis=2,...]
  transfers between devices with their start and end apart: 7 -> 0, of which waited for: 6 -> 0; matrix products, arithmetic and copies ran while one was open for 5% -> 0% of each run, Pallas kernels for 0% -> 0%
where the time goes in v1:
time: 253 us
  Pallas kernels  199 us (79%)
  matrix products  39.3 us (16%)
  other arithmetic  8.36 us (3%)
  local copies, waits for them, and re-layouts  4.9 us (2%)
    pallas_call x3, Pallas kernels, gather(): pl.pallas_call(functools.partial(gather_kernel, chips), out_shape=jax.Sha...  93.8 us
    pallas_call x3, Pallas kernels, scatter(): pl.pallas_call(functools.partial(scatter_kernel, chips), out_shape=jax.Sh...  83.5 us
    dot_general x1, matrix products, on_device(): gate = jnp.dot(normed_two, w_gate, preferred_element_type=jnp.float32)  13.2 us
    pallas_call x1, Pallas kernels, attend(): pl.pallas_call(attend_kernel, grid_spec=pltpu.PrefetchScalarGridSpec(num_...  12.1 us
    dot_general x1, matrix products, on_device(): upward = jnp.dot(normed_two, w_up, preferred_element_type=jnp.float32)  9.67 us
    pallas_call x1, Pallas kernels, joint_factor(): pl.pallas_call(functools.partial(factor_kernel, size), out_shape=jax.Shap...  9.31 us
    dot_general x1, matrix products, on_device(): jnp.dot(normed, query_key_value_weight, preferred_element_type=jnp.float32)  6.98 us
    dot_general x1, matrix products, on_device(): jnp.dot(active, w_down, preferred_element_type=jnp.float32)  5.36 us

profile of v1, /device:TPU:0, one launch (start us, length us, event | category | flops | bytes accessed | tf_op | source)
XLA Modules:
  0.0 253.0 jit_solution(3926076659654131035)
XLA Ops:
  1.3 0.1 pad_add_fusion.info_ref
  1.4 1.1 fusion.6
  2.5 1.9 fusion.8.x_ref
  4.4 31.5 %gather0.1 = bf16[8,32,5120]{2,1,0:T(8,128)(2,1)} custom-call(bf16[32,5120]{1,0:T(8,128)(2,1)} %fusion.8.x_ref), custom_call_target="tpu_custom_call" | custom-call | tf_op jit(solution)/shard_map/gather0/pallas_call | solution.py:154
  35.9 7.0 %fusion.1.x_ref = bf16[256,768]{1,0:T(8,128)(2,1)} fusion(bf16[256,5120]{1,0:T(8,128)(2,1)} %bitcast.63, bf16[5120,768]{1,0:T(8,128)(2,1)} %param.15, f32[768]{0:T(1024)S(1)} %convert_element_type.68), kind=kOutput, calls=%fused_computation.6 | convolution fusion | flops 2013659136 | bytes 10882048 | tf_op jit(solution)/shard_map/dot_general | solution.py:474
  42.9 33.3 %gather1.1 = bf16[8,256,768]{2,1,0:T(8,128)(2,1)} custom-call(bf16[256,768]{1,0:T(8,128)(2,1)} %fusion.1.x_ref), custom_call_target="tpu_custom_call" | custom-call | tf_op jit(solution)/shard_map/gather1/pallas_call | solution.py:154
  76.2 2.3 copy.19
  78.6 0.1 fusion.18
  78.8 0.5 multiply_cosine_fusion
  79.3 0.1 fusion.14
  79.4 0.1 maximum_multiply_fusion
  79.5 0.1 fusion.12.kn_ref
  79.6 0.1 pad_maximum_fusion
  79.7 0.1 copy-done.1
  79.8 0.3 copy-done.2
  80.1 12.1 %attend.1 = (bf16[8,144,1024]{2,1,0:T(8,128)(2,1)S(1)}, f32[8,1024]{1,0:T(8,128)S(1)}) custom-call(s32[2]{0:T(128)S(1)} %pad_add_fusion.info_ref, bf16[256,6144]{1,0:T(8,128)(2,1)S(1)} %bitcast.53, bf16[512,1024]{1,0:T(8,128)(2,1)S(1)} %bitcast.56, bf16[512,1024]{1,0:T(8,128)(2,1)S(1)} %bitcast.57, bf16[32,1024]{1,0:T(8,128)(2,1)S(1)} %fusion.12.kn_ref, ...), custom_call_target="tpu_custom_call" | custom-call | tf_op jit(solution)/shard_map/attend/pallas_call | solution.py:414
  92.2 1.4 copy-done
  93.6 0.6 copy-done.5
  94.3 9.3 %factor2.1 = f32[8,1024]{1,0:T(8,128)} custom-call(f32[8,1024]{1,0:T(8,128)} %copy-done.5), custom_call_target="tpu_custom_call" | custom-call | tf_op jit(solution)/shard_map/factor2/pallas_call | solution.py:350
  103.6 2.4 multiply_convert_fusion.x_ref
  106.0 26.1 %scatter3.1 = f32[144,1024]{1,0:T(8,128)S(1)} custom-call(bf16[8,144,1024]{2,1,0:T(8,128)(2,1)S(1)} %multiply_convert_fusion.x_ref), custom_call_target="tpu_custom_call" | custom-call | tf_op jit(solution)/shard_map/scatter3/pallas_call | solution.py:290
  132.1 4.0 %convolution_convert_fusion.1 = bf16[256,5120]{1,0:T(8,128)(2,1)S(1)} fusion(bf16[256,512]{0,1:T(8,128)(2,1)S(1)} %bitcast.66, bf16[512,5120]{1,0:T(8,128)(2,1)} %param.19), kind=kOutput, calls=%fused_computation.1 | convolution fusion | flops 1343488000 | bytes 8126464 | tf_op jit(solution)/shard_map/dot_general | solution.py:503
  136.2 28.6 %scatter4.1 = f32[32,5120]{1,0:T(8,128)S(1)} custom-call(bf16[8,32,5120]{2,1,0:T(8,128)(2,1)S(1)} %bitcast.54), custom_call_target="tpu_custom_call" | custom-call | tf_op jit(solution)/shard_map/scatter4/pallas_call | solution.py:290
  164.8 0.2 fusion.2
  165.0 0.9 fusion.4.x_ref
  165.9 29.0 %gather5.1 = bf16[8,32,5120]{2,1,0:T(8,128)(2,1)} custom-call(bf16[32,5120]{1,0:T(8,128)(2,1)} %fusion.4.x_ref), custom_call_target="tpu_custom_call" | custom-call | tf_op jit(solution)/shard_map/gather5/pallas_call | solution.py:154
  194.9 0.0 slice-start
  195.0 13.2 %fusion.19 = f32[256,1728]{0,1:T(8,128)} fusion(bf16[256,5120]{1,0:T(8,128)(2,1)} %bitcast.64, bf16[5120,1728]{0,1:T(8,128)(2,1)} %param.21), kind=kOutput, calls=%fused_computation.47 | convolution fusion | flops 4529848320 | bytes 22085632 | tf_op jit(solution)/shard_map/dot_general | solution.py:507
  208.2 9.7 %fusion = bf16[256,1728]{0,1:T(8,128)(2,1)S(1)} fusion(bf16[256,5120]{1,0:T(8,128)(2,1)S(1)} %bitcast.65, bf16[5120,1728]{0,1:T(8,128)(2,1)} %param.22, f32[256,1728]{0,1:T(8,128)} %fusion.19), kind=kOutput, calls=%fused_computation.4 | convolution fusion | flops 4532502528 | bytes 22970368 | tf_op jit(solution)/shard_map/dot_general | solution.py:508
  217.9 5.4 %convolution_convert_fusion = bf16[256,5120]{1,0:T(8,128)(2,1)S(1)} fusion(bf16[256,1728]{0,1:T(8,128)(2,1)S(1)} %fusion, bf16[1728,5120]{1,0:T(8,128)(2,1)S(1)} %bitcast.61), kind=kOutput, calls=%fused_computation | convolution fusion | flops 4531159040 | bytes 21200896 | tf_op jit(solution)/shard_map/dot_general | solution.py:511
  223.3 28.9 %scatter6.1 = f32[32,5120]{1,0:T(8,128)S(1)} custom-call(bf16[8,32,5120]{2,1,0:T(8,128)(2,1)S(1)} %bitcast.55), custom_call_target="tpu_custom_call" | custom-call | tf_op jit(solution)/shard_map/scatter6/pallas_call | solution.py:290
  252.2 0.8 fusion.10
  (37 shorter events, 0.2 us)
Async XLA Ops:
  0.6 35.3 %copy-start.9 = (bf16[768]{0:T(1024)(128)(2,1)S(1)}, bf16[768]{0:T(1024)(128)(2,1)}, u32[]{:S(2)}) copy-start(bf16[768]{0:T(1024)(128)(2,1)} %param.16) | copy-start | bytes 4612
  78.5 1.3 copy-start.1
  78.5 1.6 copy-start.2
  78.6 13.6 %copy-start.3 = (bf16[32,1024]{1,0:T(8,128)(2,1)}, bf16[32,1024]{1,0:T(8,128)(2,1)S(1)}, u32[]{:S(2)}) copy-start(bf16[32,1024]{1,0:T(8,128)(2,1)S(1)} %get-tuple-element.9.vn_ref) | copy-start | bytes 196612
  79.6 12.6 %copy-start.4 = (bf16[32,1024]{1,0:T(8,128)(2,1)}, bf16[32,1024]{1,0:T(8,128)(2,1)S(1)}, u32[]{:S(2)}) copy-start(bf16[32,1024]{1,0:T(8,128)(2,1)S(1)} %fusion.12.kn_ref) | copy-start | bytes 196612
  92.2 1.4 copy-start
  93.6 0.6 copy-start.5
  136.2 28.6 %copy-start.6 = (bf16[1,32,5120]{2,1,0:T(8,128)(2,1)S(1)}, bf16[1,32,5120]{2,1,0:T(8,128)(2,1)}, u32[]{:S(2)}) copy-start(bf16[1,32,5120]{2,1,0:T(8,128)(2,1)} %param.12) | copy-start | bytes 983044
  136.2 28.8 %copy-start.8 = (f32[5120]{0:T(1024)S(1)}, f32[5120]{0:T(1024)}, u32[]{:S(2)}) copy-start(f32[5120]{0:T(1024)} %param.20) | copy-start | bytes 61444
  194.9 13.3 %copy-start.7 = (bf16[8,32,5120]{2,1,0:T(8,128)(2,1)S(1)}, bf16[8,32,5120]{2,1,0:T(8,128)(2,1)}, u32[]{:S(2)}) copy-start(bf16[8,32,5120]{2,1,0:T(8,128)(2,1)} %gather5.1) | copy-start | bytes 7864324
  194.9 23.0 %slice-start = ((s8[17694720]{0:T(1024)(128)(4,1)}), s8[4194304]{0:T(1024)(128)(4,1)S(1)}, s32[]{:S(2)}) async-start(s8[17694720]{0:T(1024)(128)(4,1)} %bitcast.60), calls=%async_computation | async-start | bytes 8388608
  194.9 23.0 %slice-start.1 = ((s8[17694720]{0:T(1024)(128)(4,1)}), s8[4194304]{0:T(1024)(128)(4,1)S(1)}, s32[]{:S(2)}) async-start(s8[17694720]{0:T(1024)(128)(4,1)} %bitcast.60), calls=%async_computation.1 | async-start | bytes 8388608
  194.9 22.9 %slice-start.2 = ((s8[17694720]{0:T(1024)(128)(4,1)}), s8[4194304]{0:T(1024)(128)(4,1)S(1)}, s32[]{:S(2)}) async-start(s8[17694720]{0:T(1024)(128)(4,1)} %bitcast.60), calls=%async_computation.2 | async-start | bytes 8388608
  208.2 9.7 %slice-start.3 = ((s8[17694720]{0:T(1024)(128)(4,1)}), s8[4194304]{0:T(1024)(128)(4,1)S(1)}, s32[]{:S(2)}) async-start(s8[17694720]{0:T(1024)(128)(4,1)} %bitcast.60), calls=%async_computation.3 | async-start | bytes 8388608
  208.2 9.7 %slice-start.4 = ((s8[17694720]{0:T(1024)(128)(4,1)}), s8[917504]{0:T(1024)(128)(4,1)S(1)}, s32[]{:S(2)}) async-start(s8[17694720]{0:T(1024)(128)(4,1)} %bitcast.60), calls=%async_computation.4 | async-start | bytes 1835008

commit v2 on v1

--- a/solution.py
+++ b/solution.py
@@ -14,6 +14,7 @@
 GROUP = QUERY_HEADS // KEY_VALUE_HEADS
 SCALE = 1.0 / math.sqrt(HEAD_WIDTH)
 TAIL = 16
+FEED_TILE = 432
 
 rope_base = 1000000.0
 MESH = pl.DeviceIdType.MESH
@@ -54,116 +55,142 @@
     pl.semaphore_wait(barrier, 1 + below + above)
 
 
-def gather_kernel(chips, x_ref, out_ref, own_sem, up_send, down_send, chip_recv, pair_send, pair_recv):
+def gather_kernel(
+    chips, pieces, x_ref, out_ref, own_sem, up_send, down_send, chip_recv, pair_send, pair_recv
+):
     me = lax.axis_index("head")
     chip = me // 2
     core = me % 2
     partner = chip * 2 + (1 - core)
     chain_barrier(chips, me, chip, partner)
 
-    def to_up(src, owner):
+    def to_up(src, owner, c):
         return pltpu.make_async_remote_copy(
             src_ref=src,
-            dst_ref=out_ref.at[owner * 2 + core],
-            send_sem=up_send.at[owner],
-            recv_sem=chip_recv.at[owner],
+            dst_ref=out_ref.at[owner * 2 + core, c],
+            send_sem=up_send.at[owner, c],
+            recv_sem=chip_recv.at[owner, c],
             device_id={"head": me + 2},
             device_id_type=MESH,
         )
 
-    def to_down(src, owner):
+    def to_down(src, owner, c):
         return pltpu.make_async_remote_copy(
             src_ref=src,
-            dst_ref=out_ref.at[owner * 2 + core],
-            send_sem=down_send.at[owner],
-            recv_sem=chip_recv.at[owner],
+            dst_ref=out_ref.at[owner * 2 + core, c],
+            send_sem=down_send.at[owner, c],
+            recv_sem=chip_recv.at[owner, c],
             device_id={"head": me - 2},
             device_id_type=MESH,
         )
 
-    def to_partner(src, owner):
+    def to_partner(src, owner, c):
         return pltpu.make_async_remote_copy(
             src_ref=src,
-            dst_ref=out_ref.at[owner * 2 + core],
-            send_sem=pair_send.at[owner],
-            recv_sem=pair_recv.at[owner],
+            dst_ref=out_ref.at[owner * 2 + core, c],
+            send_sem=pair_send.at[owner, c],
+            recv_sem=pair_recv.at[owner, c],
             device_id={"head": partner},
             device_id_type=MESH,
         )
 
-    @pl.when(chip < chips - 1)
-    def _():
-        to_up(x_ref, chip).start()
-
-    @pl.when(chip > 0)
-    def _():
-        to_down(x_ref, chip).start()
-
-    to_partner(x_ref, chip).start()
+    def begin(c, carry):
+        @pl.when(chip < chips - 1)
+        def _():
+            to_up(x_ref.at[c], chip, c).start()
+
+        @pl.when(chip > 0)
+        def _():
+            to_down(x_ref.at[c], chip, c).start()
+
+        to_partner(x_ref.at[c], chip, c).start()
+        return carry
+
+    lax.fori_loop(0, pieces, begin, 0)
     own = pltpu.make_async_copy(x_ref, out_ref.at[me], own_sem)
     own.start()
 
-    def step(s, carry):
+    def step(t, carry):
+        s = 1 + t // pieces
+        c = t % pieces
+
         @pl.when(chip - s >= 0)
         def _():
             owner = chip - s
-            held = out_ref.at[owner * 2 + core]
-            to_up(held, owner).wait_recv()
+            held = out_ref.at[owner * 2 + core, c]
+            to_up(held, owner, c).wait_recv()
 
             @pl.when(chip < chips - 1)
             def _():
-                to_up(held, owner).start()
-
-            to_partner(held, owner).start()
+                to_up(held, owner, c).start()
+
+            to_partner(held, owner, c).start()
 
         @pl.when(chip + s <= chips - 1)
         def _():
             owner = chip + s
-            held = out_ref.at[owner * 2 + core]
-            to_down(held, owner).wait_recv()
+            held = out_ref.at[owner * 2 + core, c]
+            to_down(held, owner, c).wait_recv()
 
             @pl.when(chip > 0)
             def _():
-                to_down(held, owner).start()
-
-            to_partner(held, owner).start()
-
-        return carry
-
-    lax.fori_loop(1, chips, step, 0)
+                to_down(held, owner, c).start()
+
+            to_partner(held, owner, c).start()
+
+        return carry
+
+    lax.fori_loop(0, (chips - 1) * pieces, step, 0)
     own.wait()
 
-    def finish(owner, carry):
-        to_partner(x_ref, owner).wait()
+    def finish(t, carry):
+        owner = t // pieces
+        c = t % pieces
+        to_partner(x_ref.at[c], owner, c).wait()
 
         @pl.when((chip < chips - 1) & (owner <= chip))
         def _():
-            to_up(x_ref, owner).wait_send()
+            to_up(x_ref.at[c], owner, c).wait_send()
 
         @pl.when((chip > 0) & (owner >= chip))
         def _():
-            to_down(x_ref, owner).wait_send()
-
-        return carry
-
-    lax.fori_loop(0, chips, finish, 0)
-
-
-def gather(x, size, collective_id):
+            to_down(x_ref.at[c], owner, c).wait_send()
+
+        return carry
+
+    lax.fori_loop(0, chips * pieces, finish, 0)
+
+
+def gather(x, size, pieces, collective_id):
     chips = size // 2
+    rows, width = x.shape
+    x = x.reshape(pieces, rows // pieces, width)
     return pl.pallas_call(
-        functools.partial(gather_kernel, chips),
+        functools.partial(gather_kernel, chips, pieces),
         out_shape=jax.ShapeDtypeStruct((size,) + x.shape, x.dtype),
         in_specs=[pl.BlockSpec(memory_space=pl.ANY)],
         out_specs=pl.BlockSpec(memory_space=pl.ANY),
-        scratch_shapes=[pltpu.SemaphoreType.DMA(())] + [pltpu.SemaphoreType.DMA((chips,))] * 5,
+        scratch_shapes=[pltpu.SemaphoreType.DMA(())]
+        + [pltpu.SemaphoreType.DMA((chips, pieces))] * 5,
         compiler_params=pltpu.CompilerParams(collective_id=collective_id, has_side_effects=True),
         name="gather%d" % collective_id,
-    )(x)
+    )(x).reshape(size, rows, width)
 
 
 def scatter_kernel(
-    chips, x_ref, out_ref, pair, up, down, pair_send, pair_recv, up_send, up_recv, down_send, down_recv
+    chips,
+    pieces,
+    x_ref,
+    out_ref,
+    pair,
+    up,
+    down,
+    pair_send,
+    pair_recv,
+    up_send,
+    up_recv,
+    down_send,
+    down_recv,
 ):
     me = lax.axis_index("head")
     chip = me // 2
@@ -172,32 +199,32 @@
     half = chip // (chips // 2)
     chain_barrier(chips, me, chip, partner)
 
-    def to_partner(j):
+    def to_partner(j, c):
         return pltpu.make_async_remote_copy(
-            src_ref=x_ref.at[2 * j + (1 - core)],
-            dst_ref=pair.at[j],
-            send_sem=pair_send.at[j],
-            recv_sem=pair_recv.at[j],
+            src_ref=x_ref.at[2 * j + (1 - core), c],
+            dst_ref=pair.at[j, c],
+            send_sem=pair_send.at[j, c],
+            recv_sem=pair_recv.at[j, c],
             device_id={"head": partner},
             device_id_type=MESH,
         )
 
-    def to_up(src, j):
+    def to_up(src, j, c):
         return pltpu.make_async_remote_copy(
-            src_ref=src,
-            dst_ref=up.at[j],
-            send_sem=up_send.at[j],
-            recv_sem=up_recv.at[j],
+            src_ref=src.at[j, c],
+            dst_ref=up.at[j, c],
+            send_sem=up_send.at[j, c],
+            recv_sem=up_recv.at[j, c],
             device_id={"head": me + 2},
             device_id_type=MESH,
         )
 
-    def to_down(src, j):
+    def to_down(src, j, c):
         return pltpu.make_async_remote_copy(
-            src_ref=src,
-            dst_ref=down.at[j],
-            send_sem=down_send.at[j],
-            recv_sem=down_recv.at[j],
+            src_ref=src.at[j, c],
+            dst_ref=down.at[j, c],
+            send_sem=down_send.at[j, c],
+            recv_sem=down_recv.at[j, c],
             device_id={"head": me - 2},
             device_id_type=MESH,
         )
@@ -205,100 +232,113 @@
     def order(k):
         return (1 - half) * (chips - 1 - k) + half * k
 
-    def first(k, carry):
-        to_partner(order(k)).start()
-        return carry
-
-    lax.fori_loop(0, chips, first, 0)
-
-    def second(k, carry):
-        j = order(k)
-        to_partner(j).wait_recv()
-        pair[j] = pair[j] + x_ref[2 * j + core]
+    def first(t, carry):
+        to_partner(order(t // pieces), t % pieces).start()
+        return carry
+
+    lax.fori_loop(0, chips * pieces, first, 0)
+
+    def second(t, carry):
+        j = order(t // pieces)
+        c = t % pieces
+        to_partner(j, c).wait_recv()
+        pair[j, c] = pair[j, c] + x_ref[2 * j + core, c]
 
         @pl.when((chip == 0) & (j > 0))
         def _():
-            to_up(pair.at[j], j).start()
+            to_up(pair, j, c).start()
 
         @pl.when((chip == chips - 1) & (j < chips - 1))
         def _():
-            to_down(pair.at[j], j).start()
-
-        return carry
-
-    lax.fori_loop(0, chips, second, 0)
-
-    def move_up(j):
+            to_down(pair, j, c).start()
+
+        return carry
+
+    lax.fori_loop(0, chips * pieces, second, 0)
+
+    def move_up(j, c):
         @pl.when((chip > 0) & (j > chip))
         def _():
-            to_up(up.at[j], j).wait_recv()
-            up[j] = up[j] + pair[j]
-            to_up(up.at[j], j).start()
-
-    def move_down(j):
+            to_up(up, j, c).wait_recv()
+            up[j, c] = up[j, c] + pair[j, c]
+            to_up(up, j, c).start()
+
+    def move_down(j, c):
         @pl.when((chip < chips - 1) & (j < chip))
         def _():
-            to_down(down.at[j], j).wait_recv()
-            down[j] = down[j] + pair[j]
-            to_down(down.at[j], j).start()
-
-    def third(s, carry):
+            to_down(down, j, c).wait_recv()
+            down[j, c] = down[j, c] + pair[j, c]
+            to_down(down, j, c).start()
+
+    def third(t, carry):
+        s = t // pieces
+        c = t % pieces
+
         @pl.when(half == 0)
         def _():
-            move_up(chips - 1 - s)
-
-        move_down(s)
+            move_up(chips - 1 - s, c)
+
+        move_down(s, c)
 
         @pl.when(half == 1)
         def _():
-            move_up(chips - 1 - s)
-
-        return carry
-
-    lax.fori_loop(0, chips - 1, third, 0)
-    out_ref[...] = pair[chip].astype(jnp.float32)
-
-    @pl.when(chip > 0)
-    def _():
-        to_up(up.at[chip], chip).wait_recv()
-        out_ref[...] = out_ref[...] + up[chip].astype(jnp.float32)
-
-    @pl.when(chip < chips - 1)
-    def _():
-        to_down(down.at[chip], chip).wait_recv()
-        out_ref[...] = out_ref[...] + down[chip].astype(jnp.float32)
-
-    def finish(j, carry):
-        to_partner(j).wait_send()
+            move_up(chips - 1 - s, c)
+
+        return carry
+
+    lax.fori_loop(0, (chips - 1) * pieces, third, 0)
+
+    def total(c, carry):
+        out_ref[c] = pair[chip, c].astype(jnp.float32)
+
+        @pl.when(chip > 0)
+        def _():
+            to_up(up, chip, c).wait_recv()
+            out_ref[c] = out_ref[c] + up[chip, c].astype(jnp.float32)
+
+        @pl.when(chip < chips - 1)
+        def _():
+            to_down(down, chip, c).wait_recv()
+            out_ref[c] = out_ref[c] + down[chip, c].astype(jnp.float32)
+
+        return carry
+
+    lax.fori_loop(0, pieces, total, 0)
+
+    def finish(t, carry):
+        j = t // pieces
+        c = t % pieces
+        to_partner(j, c).wait_send()
 
         @pl.when(j > chip)
         def _():
-            to_up(pair.at[j], j).wait_send()
+            to_up(pair, j, c).wait_send()
 
         @pl.when(j < chip)
         def _():
-            to_down(pair.at[j], j).wait_send()
-
-        return carry
-
-    lax.fori_loop(0, chips, finish, 0)
-
-
-def scatter(x, size, collective_id):
+            to_down(pair, j, c).wait_send()
+
+        return carry
+
+    lax.fori_loop(0, chips * pieces, finish, 0)
+
+
+def scatter(x, size, pieces, collective_id):
     chips = size // 2
-    shape = x.shape[1:]
+    rows, width = x.shape[1:]
+    shape = (pieces, rows // pieces, width)
     return pl.pallas_call(
-        functools.partial(scatter_kernel, chips),
+        functools.partial(scatter_kernel, chips, pieces),
         out_shape=jax.ShapeDtypeStruct(shape, jnp.float32),
         in_specs=[pl.BlockSpec(memory_space=pltpu.VMEM)],
         out_specs=pl.BlockSpec(memory_space=pltpu.VMEM),
         scratch_shapes=[pltpu.VMEM((chips,) + shape, x.dtype)] * 3
-        + [pltpu.SemaphoreType.DMA((chips,))] * 6,
+        + [pltpu.SemaphoreType.DMA((chips, pieces))] * 6,
         compiler_params=pltpu.CompilerParams(
             collective_id=collective_id, has_side_effects=True, vmem_limit_bytes=24 << 20
         ),
         name="scatter%d" % collective_id,
-    )(x)
+    )(x.reshape((size,) + shape)).reshape(rows, width)
 
 
 def factor_kernel(size, x_ref, out_ref, held, send_sem, recv_sem):
@@ -441,6 +481,50 @@
     )(info, qkv, key_cache, value_cache, new_keys, new_values, cosine, sine)
 
 
+def feed_kernel(x_ref, gate_ref, up_ref, down_ref, out_ref, total):
+    step = pl.program_id(0)
+    last = (((1,), (1,)), ((), ()))
+    first = (((0,), (0,)), ((), ()))
+    x = x_ref[...]
+    gate = lax.dot_general(gate_ref[...], x, last, preferred_element_type=jnp.float32)
+    upward = lax.dot_general(up_ref[...], x, last, preferred_element_type=jnp.float32)
+    active = (gate / (1.0 + jnp.exp(-gate)) * upward).astype(jnp.bfloat16)
+    part = lax.dot_general(active, down_ref[...], first, preferred_element_type=jnp.float32)
+
+    @pl.when(step == 0)
+    def _():
+        total[...] = part
+
+    @pl.when(step > 0)
+    def _():
+        total[...] = total[...] + part
+
+    @pl.when(step == pl.num_programs(0) - 1)
+    def _():
+        out_ref[...] = total[...].astype(jnp.bfloat16)
+
+
+def feed(x, w_gate, w_up, w_down):
+    tokens, model = x.shape
+    units = w_down.shape[0]
+    steps = units // FEED_TILE
+    tile = units // steps
+    weight = pl.BlockSpec((tile, model), lambda i: (i, 0))
+    whole = pl.BlockSpec((tokens, model), lambda i: (0, 0))
+    return pl.pallas_call(
+        feed_kernel,
+        grid=(steps,),
+        in_specs=[whole, weight, weight, weight],
+        out_specs=whole,
+        out_shape=jax.ShapeDtypeStruct((tokens, model), jnp.bfloat16),
+        scratch_shapes=[pltpu.VMEM((tokens, model), jnp.float32)],
+        compiler_params=pltpu.CompilerParams(
+            dimension_semantics=("arbitrary",), vmem_limit_bytes=56 << 20
+        ),
+        name="feed",
+    )(x, jnp.transpose(w_gate), jnp.transpose(w_up), w_down)
+
+
 def on_device(
     hidden,
     cached_len,
@@ -464,17 +548,19 @@
     row_start = index_here * fresh
     cache_length = key_cache.shape[1]
     key_start = QUERY_HEADS * HEAD_WIDTH
+    fine = max(fresh // 8, 1)
+    coarse = max(fresh // 16, 1)
 
     cosine, sine = rope_tables(cached_len[0] + jnp.arange(tokens, dtype=jnp.int32))
     own_cosine = lax.dynamic_slice_in_dim(cosine, row_start, fresh, 0)[:, None, :]
     own_sine = lax.dynamic_slice_in_dim(sine, row_start, fresh, 0)[:, None, :]
 
-    normed = gather(rms_norm(own_rows, attn_gain), size, 0).reshape(tokens, model)
+    normed = gather(rms_norm(own_rows, attn_gain), size, fine, 0).reshape(tokens, model)
     qkv_part = (
         jnp.dot(normed, query_key_value_weight, preferred_element_type=jnp.float32)
         + b_qkv.astype(jnp.float32)
     ).astype(jnp.bfloat16)
-    qkv = jnp.transpose(gather(qkv_part, size, 1), (1, 0, 2)).reshape(tokens, -1)
+    qkv = jnp.transpose(gather(qkv_part, size, 4, 1), (1, 0, 2)).reshape(tokens, -1)
     own = lax.dynamic_slice(
         qkv, (row_start, key_start), (fresh, 2 * KEY_VALUE_HEADS * HEAD_WIDTH)
     )
@@ -496,20 +582,16 @@
     sums = jnp.transpose(
         sums.reshape(KEY_VALUE_HEADS, HEAD_WIDTH + TAIL, split, width), (0, 2, 1, 3)
     ).reshape(size, HEAD_WIDTH + TAIL, width)
-    mixed = scatter(sums, size, 3)
+    mixed = scatter(sums, size, 3, 3)
     attn = (mixed[:HEAD_WIDTH] / mixed[HEAD_WIDTH : HEAD_WIDTH + 1]).astype(jnp.bfloat16)
     attn = jnp.transpose(attn.reshape(HEAD_WIDTH, heads_here, tokens), (2, 1, 0))
     attn = attn.reshape(tokens, heads_here * HEAD_WIDTH)
     projected = jnp.dot(attn, w_out, preferred_element_type=jnp.float32).astype(jnp.bfloat16)
-    projected = scatter(projected.reshape(size, fresh, model), size, 4)
+    projected = scatter(projected.reshape(size, fresh, model), size, coarse, 4)
     middle = (own_rows.astype(jnp.float32) + projected).astype(jnp.bfloat16)
-    normed_two = gather(rms_norm(middle, ffn_gain), size, 5).reshape(tokens, model)
-    gate = jnp.dot(normed_two, w_gate, preferred_element_type=jnp.float32)
-    upward = jnp.dot(normed_two, w_up, preferred_element_type=jnp.float32)
-    active = (jax.nn.silu(gate) * upward).astype(jnp.bfloat16)
-    active = lax.optimization_barrier(active)
-    ffn_part = jnp.dot(active, w_down, preferred_element_type=jnp.float32).astype(jnp.bfloat16)
-    ffn_sum = scatter(ffn_part.reshape(size, fresh, model), size, 6)
+    normed_two = gather(rms_norm(middle, ffn_gain), size, fine, 5).reshape(tokens, model)
+    ffn_part = feed(normed_two, w_gate, w_up, w_down)
+    ffn_sum = scatter(ffn_part.reshape(size, fresh, model), size, coarse, 6)
     result = (middle.astype(jnp.float32) + ffn_sum).astype(jnp.bfloat16)
     return (result[None], new_keys[None], new_values[None])
 

time: 253 us -> 241 us (0.953)
  matrix products: 39.3 us -> 11 us
  Pallas kernels: 199 us -> 212 us
    dot_general x3 -> x0, matrix products: 28.3 us -> none  [the longest x1 13.2 us: on_device(): gate = jnp.dot(normed_two, w_gate, preferred_element_type=jnp.float32)]
    pallas_call x6 -> x7, Pallas kernels: 177 us -> 190 us  [the longest x3 88.3 us: gather(): pl.pallas_call(functools.partial(gather_kernel, chips, pieces), out_shape...]
    unnamed x31 -> x23, local copies, waits for them, and re-layouts: 2.5 us -> 6.65 us
where the time goes in v2:
time: 241 us; the launch traced here: 240 us
  Pallas kernels  212 us (88%)
  matrix products  11 us (5%)
  other arithmetic  8.42 us (3%)
  local copies, waits for them, and re-layouts  7.11 us (3%)
    pallas_call x3, Pallas kernels, gather(): pl.pallas_call(functools.partial(gather_kernel, chips, pieces), out_shape...  88.3 us
    pallas_call x3, Pallas kernels, scatter(): pl.pallas_call(functools.partial(scatter_kernel, chips, pieces), out_shap...  73.7 us
    pallas_call x1, Pallas kernels, feed(): pl.pallas_call(feed_kernel, grid=(steps,), in_specs=[whole, weight, weigh...  28.2 us
    pallas_call x1, Pallas kernels, attend(): pl.pallas_call(attend_kernel, grid_spec=pltpu.PrefetchScalarGridSpec(num_...  12.1 us
    pallas_call x1, Pallas kernels, joint_factor(): pl.pallas_call(functools.partial(factor_kernel, size), out_shape=jax.Shap...  9.91 us
    dot_general x1, matrix products, on_device(): jnp.dot(normed, query_key_value_weight, preferred_element_type=jnp.float32)  6.98 us
    unnamed x23, local copies, waits for them, and re-layouts  6.65 us

profile of v2, /device:TPU:0, one launch (start us, length us, event | category | flops | bytes accessed | tf_op | source)
XLA Modules:
  0.0 240.4 jit_solution(17165967830607588625)
XLA Ops:
  1.4 1.1 multiply_reduce_fusion.1
  2.5 0.1 rsqrt.23
  2.6 1.9 fusion.4.x_ref
  4.5 28.4 %gather0.1 = bf16[8,4,8,5120]{3,2,1,0:T(8,128)(2,1)} custom-call(bf16[4,8,5120]{2,1,0:T(8,128)(2,1)} %fusion.4.x_ref), custom_call_target="tpu_custom_call" | custom-call | tf_op jit(solution)/shard_map/gather0/pallas_call | solution.py:168
  32.9 7.0 %fusion = bf16[256,768]{1,0:T(8,128)(2,1)} fusion(bf16[256,5120]{1,0:T(8,128)(2,1)} %bitcast.88, bf16[5120,768]{1,0:T(8,128)(2,1)} %param.15, f32[768]{0:T(1024)S(1)} %convert_element_type.92), kind=kOutput, calls=%fused_computation.3 | convolution fusion | flops 2013659136 | bytes 10882048 | tf_op jit(solution)/shard_map/dot_general | solution.py:560
  39.9 30.6 %gather1.1 = bf16[8,4,64,768]{3,2,1,0:T(8,128)(2,1)} custom-call(bf16[4,64,768]{2,1,0:T(8,128)(2,1)} %bitcast.94), custom_call_target="tpu_custom_call" | custom-call | tf_op jit(solution)/shard_map/gather1/pallas_call | solution.py:168
  70.5 2.3 copy.21
  72.9 0.1 fusion.12
  73.0 0.5 multiply_cosine_fusion
  73.5 0.1 fusion.9
  73.6 0.1 maximum_multiply_fusion
  73.8 0.1 pad_maximum_fusion
  74.0 0.3 copy-done.3
  74.3 12.1 %attend.1 = (bf16[8,144,1024]{2,1,0:T(8,128)(2,1)S(1)}, f32[8,1024]{1,0:T(8,128)S(1)}) custom-call(s32[2]{0:T(128)S(1)} %pad_add_fusion.info_ref, bf16[256,6144]{1,0:T(8,128)(2,1)S(1)} %bitcast.70, bf16[512,1024]{1,0:T(8,128)(2,1)S(1)} %bitcast.79, bf16[512,1024]{1,0:T(8,128)(2,1)S(1)} %bitcast.80, bf16[32,1024]{1,0:T(8,128)(2,1)S(1)} %fusion.7.kn_ref, ...), custom_call_target="tpu_custom_call" | custom-call | tf_op jit(solution)/shard_map/attend/pallas_call | solution.py:454
  86.5 1.4 copy-done.1
  87.9 0.6 copy-done.6
  88.5 9.9 %factor2.1 = f32[8,1024]{1,0:T(8,128)} custom-call(f32[8,1024]{1,0:T(8,128)} %copy-done.6), custom_call_target="tpu_custom_call" | custom-call | tf_op jit(solution)/shard_map/factor2/pallas_call | solution.py:390
  98.4 2.3 multiply_convert_fusion
  100.7 23.3 %scatter3.1 = f32[3,48,1024]{2,1,0:T(8,128)S(1)} custom-call(bf16[8,3,48,1024]{3,2,1,0:T(8,128)(2,1)S(1)} %bitcast.75), custom_call_target="tpu_custom_call" | custom-call | tf_op jit(solution)/shard_map/scatter3/pallas_call | solution.py:330
  124.0 0.2 copy.20
  124.3 0.2 divide_convert_fusion
  124.5 0.1 copy.19
  124.6 4.0 %convolution_convert_fusion = bf16[256,5120]{1,0:T(8,128)(2,1)S(1)} fusion(bf16[256,512]{0,1:T(8,128)(2,1)S(1)} %bitcast.89, bf16[512,5120]{1,0:T(8,128)(2,1)} %param.19), kind=kOutput, calls=%fused_computation | convolution fusion | flops 1343488000 | bytes 8126464 | tf_op jit(solution)/shard_map/dot_general | solution.py:589
  128.7 26.7 %scatter4.1 = f32[2,16,5120]{2,1,0:T(8,128)S(1)} custom-call(bf16[8,2,16,5120]{3,2,1,0:T(8,128)(2,1)S(1)} %bitcast.72), custom_call_target="tpu_custom_call" | custom-call | tf_op jit(solution)/shard_map/scatter4/pallas_call | solution.py:330
  155.4 0.2 multiply_reduce_fusion
  155.6 0.1 rsqrt.25
  155.7 0.9 multiply_convert_fusion.1.x_ref
  156.6 29.4 %gather5.1 = bf16[8,4,8,5120]{3,2,1,0:T(8,128)(2,1)} custom-call(bf16[4,8,5120]{2,1,0:T(8,128)(2,1)} %multiply_convert_fusion.1.x_ref), custom_call_target="tpu_custom_call" | custom-call | tf_op jit(solution)/shard_map/gather5/pallas_call | solution.py:168
  185.9 28.2 %feed.1 = bf16[256,5120]{1,0:T(8,128)(2,1)} custom-call(bf16[256,5120]{1,0:T(8,128)(2,1)} %bitcast.86, bf16[1728,5120]{1,0:T(8,128)(2,1)} %bitcast.83, bf16[1728,5120]{1,0:T(8,128)(2,1)} %bitcast.84, bf16[1728,5120]{1,0:T(8,128)(2,1)} %down_ref.1), custom_call_target="tpu_custom_call" | custom-call | tf_op jit(solution)/shard_map/feed/pallas_call | solution.py:514
  214.2 1.7 copy-done
  215.9 23.7 %scatter6.1 = f32[2,16,5120]{2,1,0:T(8,128)S(1)} custom-call(bf16[8,2,16,5120]{3,2,1,0:T(8,128)(2,1)S(1)} %bitcast.71), custom_call_target="tpu_custom_call" | custom-call | tf_op jit(solution)/shard_map/scatter6/pallas_call | solution.py:330
  239.6 0.8 fusion.1
  (28 shorter events, 0.4 us)
Async XLA Ops:
  0.6 32.3 %copy-start.9 = (bf16[768]{0:T(1024)(128)(2,1)S(1)}, bf16[768]{0:T(1024)(128)(2,1)}, u32[]{:S(2)}) copy-start(bf16[768]{0:T(1024)(128)(2,1)} %param.16) | copy-start | bytes 4612
  72.8 1.3 copy-start.2
  72.8 1.6 copy-start.3
  72.8 13.6 %copy-start.4 = (bf16[32,1024]{1,0:T(8,128)(2,1)}, bf16[32,1024]{1,0:T(8,128)(2,1)S(1)}, u32[]{:S(2)}) copy-start(bf16[32,1024]{1,0:T(8,128)(2,1)S(1)} %get-tuple-element.7.vn_ref) | copy-start | bytes 196612
  73.8 12.6 %copy-start.5 = (bf16[32,1024]{1,0:T(8,128)(2,1)}, bf16[32,1024]{1,0:T(8,128)(2,1)S(1)}, u32[]{:S(2)}) copy-start(bf16[32,1024]{1,0:T(8,128)(2,1)S(1)} %fusion.7.kn_ref) | copy-start | bytes 196612
  86.4 1.4 copy-start.1
  87.9 0.6 copy-start.6
  128.7 26.8 %copy-start.7 = (bf16[1,32,5120]{2,1,0:T(8,128)(2,1)S(1)}, bf16[1,32,5120]{2,1,0:T(8,128)(2,1)}, u32[]{:S(2)}) copy-start(bf16[1,32,5120]{2,1,0:T(8,128)(2,1)} %param.12) | copy-start | bytes 983044
  128.7 27.0 %copy-start.8 = (f32[5120]{0:T(1024)S(1)}, f32[5120]{0:T(1024)}, u32[]{:S(2)}) copy-start(f32[5120]{0:T(1024)} %param.20) | copy-start | bytes 61444
  214.2 1.7 copy-start

commit v3 on v2

--- a/solution.py
+++ b/solution.py
@@ -15,6 +15,7 @@
 SCALE = 1.0 / math.sqrt(HEAD_WIDTH)
 TAIL = 16
 FEED_TILE = 432
+FEED_COLUMNS = 1024
 
 rope_base = 1000000.0
 MESH = pl.DeviceIdType.MESH
@@ -168,16 +169,54 @@
     return pl.pallas_call(
         functools.partial(gather_kernel, chips, pieces),
         out_shape=jax.ShapeDtypeStruct((size,) + x.shape, x.dtype),
-        in_specs=[pl.BlockSpec(memory_space=pl.ANY)],
-        out_specs=pl.BlockSpec(memory_space=pl.ANY),
+        in_specs=[pl.BlockSpec(memory_space=pltpu.VMEM)],
+        out_specs=pl.BlockSpec(memory_space=pltpu.VMEM),
         scratch_shapes=[pltpu.SemaphoreType.DMA(())]
         + [pltpu.SemaphoreType.DMA((chips, pieces))] * 5,
-        compiler_params=pltpu.CompilerParams(collective_id=collective_id, has_side_effects=True),
+        compiler_params=pltpu.CompilerParams(
+            collective_id=collective_id, has_side_effects=True, vmem_limit_bytes=16 << 20
+        ),
         name="gather%d" % collective_id,
     )(x).reshape(size, rows, width)
 
 
+def add_blocks(a, b):
+    return a.astype(jnp.float32) + b.astype(jnp.float32)
+
+
+def pack_sums(sums, total, top):
+    def narrow(v):
+        return v.astype(jnp.bfloat16).astype(jnp.float32)
+
+    total_high = narrow(total)
+    top_high = narrow(top)
+    top_middle = narrow(top - top_high)
+    rows = [total_high, total - total_high, top_high, top_middle, top - top_high - top_middle]
+    index = lax.broadcasted_iota(jnp.int32, (TAIL, sums.shape[1]), 0)
+    tail = jnp.zeros((TAIL, sums.shape[1]), jnp.float32)
+    for place, row in enumerate(rows):
+        tail = jnp.where(index == place, row, tail)
+    return jnp.concatenate([sums, tail], axis=0)
+
+
+def join_sums(a, b):
+    def unpack(block):
+        block = block.astype(jnp.float32)
+        tail = block[HEAD_WIDTH:]
+        return block[:HEAD_WIDTH], tail[0:1] + tail[1:2], (tail[2:3] + tail[3:4]) + tail[4:5]
+
+    sums_a, total_a, top_a = unpack(a)
+    sums_b, total_b, top_b = unpack(b)
+    top = jnp.maximum(top_a, top_b)
+    scale_a = jnp.exp((top_a - top) * SCALE)
+    scale_b = jnp.exp((top_b - top) * SCALE)
+    return pack_sums(
+        sums_a * scale_a + sums_b * scale_b, total_a * scale_a + total_b * scale_b, top
+    )
+
+
 def scatter_kernel(
+    join,
     chips,
     pieces,
     x_ref,
@@ -242,7 +281,7 @@
         j = order(t // pieces)
         c = t % pieces
         to_partner(j, c).wait_recv()
-        pair[j, c] = pair[j, c] + x_ref[2 * j + core, c]
+        pair[j, c] = join(pair[j, c], x_ref[2 * j + core, c]).astype(pair.dtype)
 
         @pl.when((chip == 0) & (j > 0))
         def _():
@@ -260,14 +299,14 @@
         @pl.when((chip > 0) & (j > chip))
         def _():
             to_up(up, j, c).wait_recv()
-            up[j, c] = up[j, c] + pair[j, c]
+            up[j, c] = join(up[j, c], pair[j, c]).astype(up.dtype)
             to_up(up, j, c).start()
 
     def move_down(j, c):
         @pl.when((chip < chips - 1) & (j < chip))
         def _():
             to_down(down, j, c).wait_recv()
-            down[j, c] = down[j, c] + pair[j, c]
+            down[j, c] = join(down[j, c], pair[j, c]).astype(down.dtype)
             to_down(down, j, c).start()
 
     def third(t, carry):
@@ -294,12 +333,12 @@
         @pl.when(chip > 0)
         def _():
             to_up(up, chip, c).wait_recv()
-            out_ref[c] = out_ref[c] + up[chip, c].astype(jnp.float32)
+            out_ref[c] = join(out_ref[c], up[chip, c])
 
         @pl.when(chip < chips - 1)
         def _():
             to_down(down, chip, c).wait_recv()
-            out_ref[c] = out_ref[c] + down[chip, c].astype(jnp.float32)
+            out_ref[c] = join(out_ref[c], down[chip, c])
 
         return carry
 
@@ -323,12 +362,12 @@
     lax.fori_loop(0, chips * pieces, finish, 0)
 
 
-def scatter(x, size, pieces, collective_id):
+def scatter(x, size, join, collective_id):
     chips = size // 2
-    rows, width = x.shape[1:]
-    shape = (pieces, rows // pieces, width)
+    shape = x.shape[1:]
+    pieces = shape[0]
     return pl.pallas_call(
-        functools.partial(scatter_kernel, chips, pieces),
+        functools.partial(scatter_kernel, join, chips, pieces),
         out_shape=jax.ShapeDtypeStruct(shape, jnp.float32),
         in_specs=[pl.BlockSpec(memory_space=pltpu.VMEM)],
         out_specs=pl.BlockSpec(memory_space=pltpu.VMEM),
@@ -338,71 +377,10 @@
             collective_id=collective_id, has_side_effects=True, vmem_limit_bytes=24 << 20
         ),
         name="scatter%d" % collective_id,
-    )(x.reshape((size,) + shape)).reshape(rows, width)
-
-
-def factor_kernel(size, x_ref, out_ref, held, send_sem, recv_sem):
-    me = lax.axis_index("head")
-    barrier = pltpu.get_barrier_semaphore()
-
-    def greet(k, carry):
-        pl.semaphore_signal(
-            barrier, inc=1, device_id={"head": (me + k) % size}, device_id_type=MESH
-        )
-        return carry
-
-    lax.fori_loop(1, size, greet, 0)
-    pl.semaphore_wait(barrier, size - 1)
-
-    def copy(slot, other):
-        return pltpu.make_async_remote_copy(
-            src_ref=x_ref,
-            dst_ref=held.at[slot],
-            send_sem=send_sem.at[other],
-            recv_sem=recv_sem.at[slot],
-            device_id={"head": other},
-            device_id_type=MESH,
-        )
-
-    def start(k, carry):
-        copy(me, (me + k) % size).start()
-        return carry
-
-    lax.fori_loop(1, size, start, 0)
-
-    def collect(k, best):
-        other = (me + k) % size
-        copy(other, other).wait_recv()
-        return jnp.maximum(best, held[other])
-
-    own = x_ref[...]
-    best = lax.fori_loop(1, size, collect, own)
-    out_ref[...] = jnp.exp((own - best) * SCALE)
-
-    def finish(k, carry):
-        copy(me, (me + k) % size).wait_send()
-        return carry
-
-    lax.fori_loop(1, size, finish, 0)
-
-
-def joint_factor(x, size, collective_id):
-    return pl.pallas_call(
-        functools.partial(factor_kernel, size),
-        out_shape=jax.ShapeDtypeStruct(x.shape, jnp.float32),
-        in_specs=[pl.BlockSpec(memory_space=pltpu.VMEM)],
-        out_specs=pl.BlockSpec(memory_space=pltpu.VMEM),
-        scratch_shapes=[
-            pltpu.VMEM((size,) + x.shape, x.dtype),
-            pltpu.SemaphoreType.DMA((size,)),
-            pltpu.SemaphoreType.DMA((size,)),
-        ],
-        compiler_params=pltpu.CompilerParams(collective_id=collective_id, has_side_effects=True),
-        name="factor%d" % collective_id,
     )(x)
 
 
-def attend_kernel(info_ref, q_ref, kc_ref, vc_ref, kn_ref, vn_ref, cos_ref, sin_ref, sum_ref, max_ref):
+def attend_kernel(info_ref, q_ref, kc_ref, vc_ref, kn_ref, vn_ref, cos_ref, sin_ref, sum_ref):
     tokens = q_ref.shape[0]
     length = kc_ref.shape[0]
     fresh = kn_ref.shape[0]
@@ -434,16 +412,15 @@
     ) + lax.dot_general(
         vn_ref[...], new.astype(jnp.bfloat16), first, preferred_element_type=jnp.float32
     )
-    sum_ref[0, :HEAD_WIDTH, :] = sums.astype(jnp.bfloat16)
-    sum_ref[0, HEAD_WIDTH:, :] = jnp.broadcast_to(total, (TAIL, width)).astype(jnp.bfloat16)
-    max_ref[pl.ds(pl.program_id(0), 1), :] = top
+    packed = pack_sums(sums, total, top).astype(jnp.bfloat16)
+    for j in range(GROUP):
+        sum_ref[0, j] = packed[:, j * tokens : (j + 1) * tokens]
 
 
 def attend(info, qkv, key_cache, value_cache, new_keys, new_values, cosine, sine):
     tokens = qkv.shape[0]
     length = key_cache.shape[0]
     fresh = new_keys.shape[0]
-    width = GROUP * tokens
 
     def head_block(rows):
         return pl.BlockSpec((rows, HEAD_WIDTH), lambda g, info: (0, g))
@@ -465,15 +442,13 @@
                 whole_block((tokens, HEAD_WIDTH)),
                 whole_block((tokens, HEAD_WIDTH)),
             ],
-            out_specs=[
-                pl.BlockSpec((1, HEAD_WIDTH + TAIL, width), lambda g, info: (g, 0, 0)),
-                whole_block((KEY_VALUE_HEADS, width)),
-            ],
+            out_specs=pl.BlockSpec(
+                (1, GROUP, HEAD_WIDTH + TAIL, tokens), lambda g, info: (g, 0, 0, 0)
+            ),
         ),
-        out_shape=[
-            jax.ShapeDtypeStruct((KEY_VALUE_HEADS, HEAD_WIDTH + TAIL, width), jnp.bfloat16),
-            jax.ShapeDtypeStruct((KEY_VALUE_HEADS, width), jnp.float32),
-        ],
+        out_shape=jax.ShapeDtypeStruct(
+            (KEY_VALUE_HEADS, GROUP, HEAD_WIDTH + TAIL, tokens), jnp.bfloat16
+        ),
         compiler_params=pltpu.CompilerParams(
             dimension_semantics=("arbitrary",), vmem_limit_bytes=32 << 20
         ),
@@ -481,27 +456,31 @@
     )(info, qkv, key_cache, value_cache, new_keys, new_values, cosine, sine)
 
 
-def feed_kernel(x_ref, gate_ref, up_ref, down_ref, out_ref, total):
+def feed_kernel(steps, x_ref, gate_ref, up_ref, down_ref, out_ref, turned, active):
     step = pl.program_id(0)
-    last = (((1,), (1,)), ((), ()))
-    first = (((0,), (0,)), ((), ()))
-    x = x_ref[...]
-    gate = lax.dot_general(gate_ref[...], x, last, preferred_element_type=jnp.float32)
-    upward = lax.dot_general(up_ref[...], x, last, preferred_element_type=jnp.float32)
-    active = (gate / (1.0 + jnp.exp(-gate)) * upward).astype(jnp.bfloat16)
-    part = lax.dot_general(active, down_ref[...], first, preferred_element_type=jnp.float32)
+    tile = gate_ref.shape[0]
 
     @pl.when(step == 0)
     def _():
-        total[...] = part
-
-    @pl.when(step > 0)
+        turned[...] = jnp.transpose(x_ref[...])
+
+    @pl.when(step < steps)
     def _():
-        total[...] = total[...] + part
-
-    @pl.when(step == pl.num_programs(0) - 1)
+        x = turned[...]
+        gate = jnp.dot(gate_ref[...], x, preferred_element_type=jnp.float32)
+        upward = jnp.dot(up_ref[...], x, preferred_element_type=jnp.float32)
+        active[pl.ds(pl.multiple_of(step * tile, tile), tile), :] = (
+            gate / (1.0 + jnp.exp(-gate)) * upward
+        ).astype(jnp.bfloat16)
+
+    @pl.when(step >= steps)
     def _():
-        out_ref[...] = total[...].astype(jnp.bfloat16)
+        out_ref[...] = lax.dot_general(
+            active[...],
+            down_ref[...],
+            (((0,), (0,)), ((), ())),
+            preferred_element_type=jnp.float32,
+        ).astype(jnp.bfloat16)
 
 
 def feed(x, w_gate, w_up, w_down):
@@ -509,17 +488,24 @@
     units = w_down.shape[0]
     steps = units // FEED_TILE
     tile = units // steps
-    weight = pl.BlockSpec((tile, model), lambda i: (i, 0))
-    whole = pl.BlockSpec((tokens, model), lambda i: (0, 0))
+    weight = pl.BlockSpec((tile, model), lambda i: (jnp.minimum(i, steps - 1), 0))
     return pl.pallas_call(
-        feed_kernel,
-        grid=(steps,),
-        in_specs=[whole, weight, weight, weight],
-        out_specs=whole,
+        functools.partial(feed_kernel, steps),
+        grid=(steps + model // FEED_COLUMNS,),
+        in_specs=[
+            pl.BlockSpec((tokens, model), lambda i: (0, 0)),
+            weight,
+            weight,
+            pl.BlockSpec((units, FEED_COLUMNS), lambda i: (0, jnp.maximum(i - steps, 0))),
+        ],
+        out_specs=pl.BlockSpec((tokens, FEED_COLUMNS), lambda i: (0, jnp.maximum(i - steps, 0))),
         out_shape=jax.ShapeDtypeStruct((tokens, model), jnp.bfloat16),
-        scratch_shapes=[pltpu.VMEM((tokens, model), jnp.float32)],
+        scratch_shapes=[
+            pltpu.VMEM((model, tokens), jnp.bfloat16),
+            pltpu.VMEM((units, tokens), jnp.bfloat16),
+        ],
         compiler_params=pltpu.CompilerParams(
-            dimension_semantics=("arbitrary",), vmem_limit_bytes=56 << 20
+            dimension_semantics=("arbitrary",), vmem_limit_bytes=48 << 20
         ),
         name="feed",
     )(x, jnp.transpose(w_gate), jnp.transpose(w_up), w_down)
@@ -548,14 +534,13 @@
     row_start = index_here * fresh
     cache_length = key_cache.shape[1]
     key_start = QUERY_HEADS * HEAD_WIDTH
-    fine = max(fresh // 8, 1)
     coarse = max(fresh // 16, 1)
 
     cosine, sine = rope_tables(cached_len[0] + jnp.arange(tokens, dtype=jnp.int32))
     own_cosine = lax.dynamic_slice_in_dim(cosine, row_start, fresh, 0)[:, None, :]
     own_sine = lax.dynamic_slice_in_dim(sine, row_start, fresh, 0)[:, None, :]
 
-    normed = gather(rms_norm(own_rows, attn_gain), size, fine, 0).reshape(tokens, model)
+    normed = gather(rms_norm(own_rows, attn_gain), size, coarse, 0).reshape(tokens, model)
     qkv_part = (
         jnp.dot(normed, query_key_value_weight, preferred_element_type=jnp.float32)
         + b_qkv.astype(jnp.float32)
@@ -572,26 +557,19 @@
     new_values = own[:, KEY_VALUE_HEADS * HEAD_WIDTH :]
 
     info = jnp.stack([cached_len[0] - index_here * cache_length, row_start]).astype(jnp.int32)
-    sums, tops = attend(
-        info, qkv, key_cache[0], value_cache[0], new_keys, new_values, cosine, sine
-    )
-    factor = joint_factor(tops, size, 2)
-    sums = (sums.astype(jnp.float32) * factor[:, None, :]).astype(jnp.bfloat16)
-    split = size // KEY_VALUE_HEADS
-    width = heads_here * tokens
-    sums = jnp.transpose(
-        sums.reshape(KEY_VALUE_HEADS, HEAD_WIDTH + TAIL, split, width), (0, 2, 1, 3)
-    ).reshape(size, HEAD_WIDTH + TAIL, width)
-    mixed = scatter(sums, size, 3, 3)
-    attn = (mixed[:HEAD_WIDTH] / mixed[HEAD_WIDTH : HEAD_WIDTH + 1]).astype(jnp.bfloat16)
-    attn = jnp.transpose(attn.reshape(HEAD_WIDTH, heads_here, tokens), (2, 1, 0))
-    attn = attn.reshape(tokens, heads_here * HEAD_WIDTH)
+    sums = attend(info, qkv, key_cache[0], value_cache[0], new_keys, new_values, cosine, sine)
+    sums = sums.reshape(size, heads_here, HEAD_WIDTH + TAIL, tokens)
+    mixed = scatter(sums, size, join_sums, 3)
+    total = mixed[:, HEAD_WIDTH : HEAD_WIDTH + 1] + mixed[:, HEAD_WIDTH + 1 : HEAD_WIDTH + 2]
+    attn = (mixed[:, :HEAD_WIDTH] / total).astype(jnp.bfloat16)
+    attn = jnp.transpose(attn, (2, 0, 1)).reshape(tokens, heads_here * HEAD_WIDTH)
     projected = jnp.dot(attn, w_out, preferred_element_type=jnp.float32).astype(jnp.bfloat16)
-    projected = scatter(projected.reshape(size, fresh, model), size, coarse, 4)
+    blocks = (size, coarse, fresh // coarse, model)
+    projected = scatter(projected.reshape(blocks), size, add_blocks, 4).reshape(fresh, model)
     middle = (own_rows.astype(jnp.float32) + projected).astype(jnp.bfloat16)
-    normed_two = gather(rms_norm(middle, ffn_gain), size, fine, 5).reshape(tokens, model)
+    normed_two = gather(rms_norm(middle, ffn_gain), size, coarse, 5).reshape(tokens, model)
     ffn_part = feed(normed_two, w_gate, w_up, w_down)
-    ffn_sum = scatter(ffn_part.reshape(size, fresh, model), size, coarse, 6)
+    ffn_sum = scatter(ffn_part.reshape(blocks), size, add_blocks, 6).reshape(fresh, model)
     result = (middle.astype(jnp.float32) + ffn_sum).astype(jnp.bfloat16)
     return (result[None], new_keys[None], new_values[None])
 

time: 241 us -> 215 us (0.89)
  Pallas kernels: 212 us -> 199 us
  local copies, waits for them, and re-layouts: 7.11 us -> 1.02 us
  matrix products: 11 us -> 7.02 us
  other arithmetic: 8.42 us -> 5.28 us
    pallas_call x5 -> x4, Pallas kernels: 112 us -> 101 us  [the longest x3 76.6 us: scatter(): pl.pallas_call(functools.partial(scatter_kernel, join, chips, pieces), ou...]
    unnamed x23, local copies, waits for them, and re-layouts: 6.65 us -> 0.83 us
    dot_general x1, matrix products: 4.04 us -> 1.55 us  [on_device(): jnp.dot(attn, w_out, preferred_element_type=jnp.float32)]
    convert_element_type x2 -> x1, other arithmetic: 2.53 us -> 0.05 us  [on_device(): attn = (mixed[:, :HEAD_WIDTH] / total).astype(jnp.bfloat16)]
    pallas_call x3, Pallas kernels: 88.3 us -> 85.9 us  [gather(): pl.pallas_call(functools.partial(gather_kernel, chips, pieces), out_shape...]
where the time goes in v3:
time: 215 us; the launch traced here: 214 us
  Pallas kernels  199 us (93%)
  matrix products  7.02 us (3%)
  other arithmetic  5.28 us (2%)
    pallas_call x3, Pallas kernels, gather(): pl.pallas_call(functools.partial(gather_kernel, chips, pieces), out_shape...  85.9 us
    pallas_call x3, Pallas kernels, scatter(): pl.pallas_call(functools.partial(scatter_kernel, join, chips, pieces), ou...  76.6 us
    pallas_call x1, Pallas kernels, feed(): pl.pallas_call(functools.partial(feed_kernel, steps), grid=(steps + model...  24.7 us
    pallas_call x1, Pallas kernels, attend(): pl.pallas_call(attend_kernel, grid_spec=pltpu.PrefetchScalarGridSpec(num_...  12.2 us
    dot_general x1, matrix products, on_device(): jnp.dot(normed, query_key_value_weight, preferred_element_type=jnp.float32)  5.47 us

profile of v3, /device:TPU:0, one launch (start us, length us, event | category | flops | bytes accessed | tf_op | source)
XLA Modules:
  0.0 214.2 jit_solution(17736992910357747015)
XLA Ops:
  0.6 1.1 multiply_reduce_fusion
  1.8 0.1 rsqrt.20
  1.9 1.9 multiply_convert_fusion
  4.5 0.1 pad_add_fusion.info_ref
  4.5 27.5 %gather0.1 = bf16[8,2,16,5120]{3,2,1,0:T(8,128)(2,1)S(1)} custom-call(bf16[2,16,5120]{2,1,0:T(8,128)(2,1)S(1)} %get-tuple-element.5.x_ref), custom_call_target="tpu_custom_call" | custom-call | tf_op jit(solution)/shard_map/gather0/pallas_call | solution.py:169
  32.0 5.5 %fusion = bf16[256,768]{1,0:T(8,128)(2,1)S(1)} fusion(bf16[256,5120]{1,0:T(8,128)(2,1)S(1)} %bitcast.63, bf16[5120,768]{1,0:T(8,128)(2,1)} %param.15, f32[768]{0:T(1024)S(1)} %convert_element_type.77), kind=kOutput, calls=%fused_computation.2 | convolution fusion | flops 2013659136 | bytes 10882048 | tf_op jit(solution)/shard_map/dot_general | solution.py:545
  37.5 30.0 %gather1.1 = bf16[8,4,64,768]{3,2,1,0:T(8,128)(2,1)S(1)} custom-call(bf16[4,64,768]{2,1,0:T(8,128)(2,1)S(1)} %bitcast.67), custom_call_target="tpu_custom_call" | custom-call | tf_op jit(solution)/shard_map/gather1/pallas_call | solution.py:169
  67.5 0.4 copy.17
  67.9 0.0 copy-start
  67.9 0.0 copy-start.1
  67.9 0.0 copy-start.2
  68.0 0.1 fusion.12
  68.1 0.5 multiply_cosine_fusion
  68.6 0.1 fusion.9
  68.7 0.1 maximum_multiply_fusion
  68.9 0.1 fusion.7.kn_ref
  68.9 0.0 copy-start.3
  68.9 0.1 pad_maximum_fusion
  69.1 0.0 slice-start
  69.1 0.0 copy-done
  69.1 0.3 copy-done.1
  69.4 12.2 %attend.1.x_ref = bf16[8,4,144,256]{3,2,1,0:T(8,128)(2,1)S(1)} custom-call(s32[2]{0:T(128)S(1)} %pad_add_fusion.info_ref, bf16[256,6144]{1,0:T(8,128)(2,1)S(1)} %bitcast.57, bf16[512,1024]{1,0:T(8,128)(2,1)S(1)} %bitcast.65, bf16[512,1024]{1,0:T(8,128)(2,1)S(1)} %bitcast.66, bf16[32,1024]{1,0:T(8,128)(2,1)S(1)} %fusion.7.kn_ref, ...), custom_call_target="tpu_custom_call" | custom-call | tf_op jit(solution)/shard_map/attend/pallas_call | solution.py:431
  81.6 23.9 %scatter3.1 = f32[4,144,256]{2,1,0:T(8,128)S(1)} custom-call(bf16[8,4,144,256]{3,2,1,0:T(8,128)(2,1)S(1)} %attend.1.x_ref), custom_call_target="tpu_custom_call" | custom-call | tf_op jit(solution)/shard_map/scatter3/pallas_call | solution.py:369
  105.6 1.5 convolution_convert_fusion
  107.2 28.9 %scatter4.1 = f32[2,16,5120]{2,1,0:T(8,128)S(1)} custom-call(bf16[8,2,16,5120]{3,2,1,0:T(8,128)(2,1)S(1)} %bitcast.61), custom_call_target="tpu_custom_call" | custom-call | tf_op jit(solution)/shard_map/scatter4/pallas_call | solution.py:369
  136.2 0.1 fusion.1
  136.3 0.0 copy-done.6
  136.3 0.2 fusion.3.x_ref
  136.5 28.5 %gather5.1 = bf16[8,2,16,5120]{3,2,1,0:T(8,128)(2,1)S(1)} custom-call(bf16[2,16,5120]{2,1,0:T(8,128)(2,1)S(1)} %fusion.3.x_ref), custom_call_target="tpu_custom_call" | custom-call | tf_op jit(solution)/shard_map/gather5/pallas_call | solution.py:169
  165.0 24.7 %feed.1 = bf16[256,5120]{1,0:T(8,128)(2,1)S(1)} custom-call(bf16[256,5120]{1,0:T(8,128)(2,1)S(1)} %bitcast.59, bf16[1728,5120]{1,0:T(8,128)(2,1)} %bitcast.70, bf16[1728,5120]{1,0:T(8,128)(2,1)} %bitcast.71, bf16[1728,5120]{1,0:T(8,128)(2,1)} %down_ref.1), custom_call_target="tpu_custom_call" | custom-call | tf_op jit(solution)/shard_map/feed/pallas_call | solution.py:492
  189.7 23.7 %scatter6.1 = f32[2,16,5120]{2,1,0:T(8,128)S(1)} custom-call(bf16[8,2,16,5120]{3,2,1,0:T(8,128)(2,1)S(1)} %bitcast.60), custom_call_target="tpu_custom_call" | custom-call | tf_op jit(solution)/shard_map/scatter6/pallas_call | solution.py:369
  213.4 0.8 fusion.4
  (24 shorter events, 0.2 us)
Async XLA Ops:
  0.6 31.4 %copy-start.7 = (bf16[768]{0:T(1024)(128)(2,1)S(1)}, bf16[768]{0:T(1024)(128)(2,1)}, u32[]{:S(2)}) copy-start(bf16[768]{0:T(1024)(128)(2,1)} %param.16) | copy-start | bytes 4612
  67.9 1.3 copy-start
  67.9 1.6 copy-start.1
  67.9 13.7 %copy-start.2 = (bf16[32,1024]{1,0:T(8,128)(2,1)}, bf16[32,1024]{1,0:T(8,128)(2,1)S(1)}, u32[]{:S(2)}) copy-start(bf16[32,1024]{1,0:T(8,128)(2,1)S(1)} %get-tuple-element.7.vn_ref) | copy-start | bytes 196612
  68.9 12.7 %copy-start.3 = (bf16[32,1024]{1,0:T(8,128)(2,1)}, bf16[32,1024]{1,0:T(8,128)(2,1)S(1)}, u32[]{:S(2)}) copy-start(bf16[32,1024]{1,0:T(8,128)(2,1)S(1)} %fusion.7.kn_ref) | copy-start | bytes 196612
  69.1 36.5 %slice-start = ((s8[5242880]{0:T(1024)(128)(4,1)}), s8[4194304]{0:T(1024)(128)(4,1)S(1)}, s32[]{:S(2)}) async-start(s8[5242880]{0:T(1024)(128)(4,1)} %bitcast.72), calls=%async_computation | async-start | bytes 8388608
  69.4 36.2 %slice-start.1 = ((s8[5242880]{0:T(1024)(128)(4,1)}), s8[1048576]{0:T(1024)(128)(4,1)S(1)}, s32[]{:S(2)}) async-start(s8[5242880]{0:T(1024)(128)(4,1)} %bitcast.72), calls=%async_computation.1 | async-start | bytes 2097152
  107.2 29.0 %copy-start.5 = (f32[2,16,5120]{2,1,0:T(8,128)S(1)}, f32[2,16,5120]{2,1,0:T(8,128)}, u32[]{:S(2)}) copy-start(f32[2,16,5120]{2,1,0:T(8,128)} %get-tuple-element.6) | copy-start | bytes 1966084
  107.2 29.1 %copy-start.6 = (f32[5120]{0:T(1024)S(1)}, f32[5120]{0:T(1024)}, u32[]{:S(2)}) copy-start(f32[5120]{0:T(1024)} %param.20) | copy-start | bytes 61444
  189.7 23.8 %copy-start.4 = (bf16[1,32,5120]{2,1,0:T(8,128)(2,1)S(1)}, bf16[1,32,5120]{2,1,0:T(8,128)(2,1)}, u32[]{:S(2)}) copy-start(bf16[1,32,5120]{2,1,0:T(8,128)(2,1)} %param.12) | copy-start | bytes 983044
